TPU v7x, 256 devices: a whole 4x4x8 slice. The times are simulated.
256 devices in a mesh: ang: 64 (over x, z, core), sy: 2 (over y_hi), sx: 2 (over y_lo).
Axes of the slice: x: 4, y: 4 (y_hi: 2, y_lo: 2; y = y_hi * 2 + y_lo), z: 8, core: 2. Of those that a mesh axis runs over, the one named last changes fastest.
Arguments:
- objects: bfloat16 [64, 2, 1024, 1024], P('ang', None, 'sy', 'sx'), may hold values from -4 to 4
- probe: float32 [2, 2, 256, 256], replicated, may hold values from -4 to 4
- data: bfloat16 [64, 2, 2, 2, 256, 256], P('ang', 'sy', 'sx'), may hold values from 0 to 4
- positions: int32 [64, 2, 2, 2, 2], P('ang', 'sy', 'sx'), may hold values from 0 to 384
- block_index: int32 [8, 16], replicated, may hold values from 0 to 511, as said below
- block_values: bfloat16 [8, 16, 128, 128], replicated, may hold values from -0.125 to 0.125
Outputs:
- object_grad: float32 [64, 2, 1024, 1024], P('ang', None, 'sy', 'sx')
- probe_grad: float32 [64, 2, 2, 256, 256], P('ang')
- vol_grad: float32 [2, 512, 2, 1024], P('sy', ('ang', 'sx'))
Inputs may be any that keep to these rules, and one draw needn't show every extreme that they name: `positions`: A position counts cells from 64 cells before the tile's first row or column. `block_index`: entry g names the angle g // 8 and the column block g % 8; every angle is named by exactly 2 entries.
All inputs are finite; a program needn't handle non-finite values.
Results may differ from a plain program's by a relative error of at most 0.011.
Values may be sent and summed in bfloat16 or wider, within the bound.
A program may use at most 64 MiB of HBM per device.

v0:
```python
from functools import partial
import math

import jax
import jax.numpy as jnp
from jax import lax
from jax.sharding import PartitionSpec as P

PATCH = 256
RIM = 64
BLK = 128


def with_halo(cells, sides, width):
    for axis, dim in sides:
        count = lax.axis_size(axis)
        ends = count - 1
        head = lax.slice_in_dim(cells, 0, width, axis=dim)
        tail = lax.slice_in_dim(cells, cells.shape[dim] - width, cells.shape[dim], axis=dim)
        cells = jnp.concatenate(
            [
                lax.ppermute(tail, axis, [(i, (i + 1) % count) for i in range(ends)]),
                cells,
                lax.ppermute(head, axis, [((i + 1) % count, i) for i in range(ends)]),
            ],
            axis=dim,
        )
    return cells


def dft_parts(length):
    sample_ids = jnp.arange(length, dtype=jnp.int32)
    product = sample_ids[:, None] * sample_ids[None, :] % length
    phases = product.astype(jnp.float32) * (2.0 * math.pi / length)
    factor = 1.0 / math.sqrt(length)
    return (jnp.cos(phases) * factor, -jnp.sin(phases) * factor)


def dft_blocks(length):
    real_part, imag_part = dft_parts(length)
    forward = jnp.stack(
        [jnp.stack([real_part, -imag_part], 1), jnp.stack([imag_part, real_part], 1)], 0
    )
    backward = jnp.stack(
        [jnp.stack([real_part, imag_part], 1), jnp.stack([-imag_part, real_part], 1)], 0
    )
    return (forward.astype(jnp.bfloat16), backward.astype(jnp.bfloat16))


def ramp_table(width):
    column_ids = jnp.arange(width, dtype=jnp.int32)
    offsets = column_ids[None, :] - column_ids[:, None]
    odd_cells = offsets % 2 != 0
    scaled = offsets.astype(jnp.float32) * math.pi
    values = jnp.where(odd_cells, -1.0 / jnp.maximum(scaled * scaled, 1.0), 0.0)
    values = jnp.where(offsets == 0, 0.25, values)
    return values.astype(jnp.bfloat16)


def left_product(matrix, fields):
    return jnp.einsum("srtk,btkc->bsrc", matrix, fields, preferred_element_type=jnp.float32)


def right_product(fields, matrix):
    return jnp.einsum("btrc,tcsq->bsrq", fields, matrix, preferred_element_type=jnp.float32)


def cut_window(field, corner):
    return lax.dynamic_slice(
        field, (jnp.int32(0), corner[0], corner[1]), (field.shape[0], PATCH, PATCH)
    )


def patch_gradients(patches, measured, probe, forward, backward):
    patch_count = patches.shape[0]
    mode_count = probe.shape[0]
    side = patches.shape[2]
    object_real = patches[:, 0].astype(jnp.float32)[:, None]
    object_imag = patches[:, 1].astype(jnp.float32)[:, None]
    probe_real = probe[None, :, 0]
    probe_imag = probe[None, :, 1]
    exit_real = probe_real * object_real - probe_imag * object_imag
    exit_imag = probe_real * object_imag + probe_imag * object_real
    exit_waves = (
        jnp.stack([exit_real, exit_imag], 2)
        .reshape(patch_count * mode_count, 2, side, side)
        .astype(jnp.bfloat16)
    )
    half_done = left_product(forward, exit_waves).astype(jnp.bfloat16)
    far_field = right_product(half_done, backward).reshape(patch_count, mode_count, 2, side, side)
    intensity = jnp.sum(far_field * far_field, axis=(1, 2))
    misfit = intensity - measured.astype(jnp.float32)
    weighted = (
        (misfit[:, None, None] * far_field)
        .reshape(patch_count * mode_count, 2, side, side)
        .astype(jnp.bfloat16)
    )
    back_half = left_product(backward, weighted).astype(jnp.bfloat16)
    spread = right_product(back_half, forward).reshape(patch_count, mode_count, 2, side, side)
    chi_real = spread[:, :, 0]
    chi_imag = spread[:, :, 1]
    grad_real = jnp.sum(probe_real * chi_real + probe_imag * chi_imag, axis=1)
    grad_imag = jnp.sum(probe_real * chi_imag - probe_imag * chi_real, axis=1)
    patch_grad = jnp.stack([grad_real, grad_imag], 1)
    probe_real_part = jnp.sum(object_real * chi_real + object_imag * chi_imag, axis=0)
    probe_imag_part = jnp.sum(object_real * chi_imag - object_imag * chi_real, axis=0)
    probe_part = jnp.stack([probe_real_part, probe_imag_part], 1)
    return (patch_grad, probe_part)


def fold_rims(field, axis_at, extent):
    inside = lax.slice_in_dim(field, 2 * RIM, 2 * RIM + extent, axis=axis_at)
    leading = lax.slice_in_dim(field, 0, RIM, axis=axis_at)
    trailing = lax.slice_in_dim(field, extent + 3 * RIM, extent + 4 * RIM, axis=axis_at)
    widths_lead = [(0, 0)] * field.ndim
    widths_lead[axis_at] = (0, extent - RIM)
    widths_trail = [(0, 0)] * field.ndim
    widths_trail[axis_at] = (extent - RIM, 0)
    return inside + jnp.pad(leading, widths_lead) + jnp.pad(trailing, widths_trail)


def body(objects, probe, data, positions, block_index, block_values):
    forward, backward = dft_blocks(PATCH)
    tile_rows = objects.shape[2]
    tile_cols = objects.shape[3]
    padded = with_halo(objects[0], (("sy", 1), ("sx", 2)), RIM)
    starts = positions[0, 0, 0]
    patches = jax.vmap(partial(cut_window, padded))(starts)
    patch_grad, probe_part = patch_gradients(patches, data[0, 0, 0], probe, forward, backward)

    def place_patch(grad_piece, corner):
        empty = jnp.zeros(padded.shape, jnp.float32)
        return lax.dynamic_update_slice(empty, grad_piece, (jnp.int32(0), corner[0], corner[1]))

    running_sum = jnp.sum(jax.vmap(place_patch)(patch_grad, starts), axis=0)
    returned = with_halo(running_sum.astype(jnp.bfloat16), (("sy", 1), ("sx", 2)), RIM).astype(
        running_sum.dtype
    )
    object_grad = fold_rims(fold_rims(returned, 1, tile_rows), 2, tile_cols)
    tile_count = lax.axis_size("sy") * lax.axis_size("sx")
    probe_total = lax.psum(probe_part.astype(jnp.bfloat16), ("sy", "sx")).astype(jnp.float32)
    probe_grad = (probe_total / math.sqrt(starts.shape[0] * tile_count))[None]
    line_blocks = block_values.shape[0]
    width_all = line_blocks * block_values.shape[2]
    angle_count = lax.axis_size("ang")
    column_parts = lax.axis_size("sx")
    rows_here = tile_rows // (angle_count * column_parts)
    ramp_matrix = ramp_table(width_all)
    sinogram = object_grad.astype(jnp.bfloat16)[None]
    ramp_split = ramp_matrix.reshape(column_parts, tile_cols, width_all)
    received = lax.all_to_all(sinogram, ("ang", "sx"), split_axis=2, concat_axis=0, tiled=True)
    shaped = received.reshape(angle_count, column_parts, received.shape[1], rows_here, tile_cols)
    result = jnp.einsum("ascrt,stv->acrv", shaped, ramp_split, preferred_element_type=jnp.float32)
    filtered = result.astype(jnp.bfloat16)
    line_data = filtered.reshape(filtered.shape[0], 2, rows_here, line_blocks, BLK)
    angle_of = block_index // line_blocks
    column_of = block_index % line_blocks
    picked = line_data[angle_of, :, :, column_of, :]
    volume = jnp.einsum(
        "bkcru,bkuv->rcbv", picked, block_values, preferred_element_type=jnp.float32
    )
    vol_grad = volume.reshape(1, rows_here, 2, width_all)
    return (object_grad[None], probe_grad, vol_grad)


def solution(mesh):
    placed = (
        P("ang", None, "sy", "sx"),
        P(),
        P("ang", "sy", "sx", None, None, None),
        P("ang", "sy", "sx", None, None),
        P(),
        P(),
    )
    return jax.shard_map(
        body,
        mesh=mesh,
        in_specs=placed,
        out_specs=(
            P("ang", None, "sy", "sx"),
            P("ang", None, None, None, None),
            P("sy", ("ang", "sx"), None, None),
        ),
        check_vma=False,
    )
```

profile of v0, /device:TPU:1, one launch (start us, length us, event | category | flops | bytes accessed | tf_op | source)
XLA Modules:
  0.0 220.0 jit_solution(13552120313437192784)
XLA Ops:
  8.3 5.6 %collective-permute-start = (bf16[2,64,512]{2,1,0:T(8,128)(2,1)S(1)}, bf16[2,64,512]{2,1,0:T(8,128)(2,1)S(1)}, u32[]{:S(2)}, u32[]{:S(2)}) collective-permute-start(bf16[2,64,512]{2,1,0:T(8,128)(2,1)S(1)} %get-tuple-element.75), channel_id=1, source_target_pairs={{0,2},{1,3},{4,6},{5,7},{8,10},{9,11},{12,14},{13,15},{16,18},{17,... | collective-permute-start | bytes 393224 | tf_op jit(solution)/shard_map/ppermute | solution.py:22
  23.5 3.0 %collective-permute-start.2 = (bf16[2,640,64]{2,1,0:T(8,128)(2,1)}, bf16[2,640,64]{2,1,0:T(8,128)(2,1)}, u32[]{:S(2)}, u32[]{:S(2)}) collective-permute-start(bf16[2,640,64]{2,1,0:T(8,128)(2,1)} %get-tuple-element.71), channel_id=1, source_target_pairs={{0,1},{2,3},{4,5},{6,7},{8,9},{10,11},{12,13},{14,15},{16,17},{18,... | collective-permute-start | bytes 491528 | tf_op jit(solution)/shard_map/ppermute | solution.py:22
  29.3 1.8 copy.54
  31.1 2.0 maximum_bitcast_fusion.3
  33.2 3.6 %collective-permute-done.3 = bf16[2,640,64]{2,1,0:T(8,128)(2,1)} collective-permute-done((bf16[2,640,64]{2,1,0:T(8,128)(2,1)}, bf16[2,640,64]{2,1,0:T(8,128)(2,1)}, u32[]{:S(2)}, u32[]{:S(2)}) %collective-permute-start.3) | collective-permute-done | bytes 163872 | tf_op jit(solution)/shard_map/ppermute | solution.py:24
  36.8 2.2 pad_maximum_fusion
  38.9 5.8 %while.2 = (s32[]{:T(128)}, bf16[2,640,640]{2,1,0:T(8,128)(2,1)S(1)}, s32[2,3]{1,0:T(2,128)S(1)}, bf16[2,2,256,256]{3,2,1,0:T(8,128)(2,1)}, s32[]{:T(128)}) while((s32[]{:T(128)}, bf16[2,640,640]{2,1,0:T(8,128)(2,1)S(1)}, s32[2,3]{1,0:T(2,128)S(1)}, bf16[2,2,256,256]{3,2,1,0:T(8,128)(2,1)}, s32[]{:T(128)}) %tuple.63), condition=%wide.while_cond, body=%wide.while_body.sunk | while | flops 2 | bytes 525929 | solution.py:69
  39.6 2.2 %bitcast_dynamic-update-slice_fusion.2 = bf16[2,2,256,256]{3,2,1,0:T(8,128)(2,1)} fusion(bf16[2,2,256,256]{3,2,1,0:T(8,128)(2,1)} %get-tuple-element.161, s32[]{:T(128)} %get-tuple-element.158, bf16[2,640,640]{2,1,0:T(8,128)(2,1)S(1)} %get-tuple-element.164, s32[]{:T(128)} %bitcast.203, s32[]{:T(128)} %bitcast.204), kind=kLoop, calls=%fused_computation.1.clone.1 | loop fusion | bytes 525824 | tf_op jit(solution)/shard_map/vmap()/gather
  42.5 2.2 %bitcast_dynamic-update-slice_fusion.2 = bf16[2,2,256,256]{3,2,1,0:T(8,128)(2,1)} fusion(bf16[2,2,256,256]{3,2,1,0:T(8,128)(2,1)} %get-tuple-element.161, s32[]{:T(128)} %get-tuple-element.158, bf16[2,640,640]{2,1,0:T(8,128)(2,1)S(1)} %get-tuple-element.164, s32[]{:T(128)} %bitcast.203, s32[]{:T(128)} %bitcast.204), kind=kLoop, calls=%fused_computation.1.clone.1 | loop fusion | bytes 525824 | tf_op jit(solution)/shard_map/vmap()/gather
  47.7 5.0 %fusion.15 = (f32[4,256,256]{1,2,0:T(8,128)}, f32[2,256,4,256,1]{3,1,4,2,0:T(8,128)}) fusion(bf16[4,1,256,256]{2,3,1,0:T(8,128)(2,1)} %bitcast.227, bf16[4,1,256,256]{2,3,1,0:T(8,128)(2,1)} %bitcast.226, bf16[1,256,2,256]{3,1,2,0:T(8,128)(2,1)S(1)} %copy-done.10, bf16[1,256,2,256]{3,1,2,0:T(8,128)(2,1)S(1)} %copy-done.9, ...), kind=kOutput, calls=%fused_computation.31 | convolution fusion | flops 1078198272 | bytes 5242880 | tf_op jit(solution)/shard_map/btrc,tcsq->bsrq/dot_general | solution.py:65
  55.2 3.4 %fusion.33 = f32[2,256,4,256,1]{3,1,4,2,0:T(8,128)S(1)} fusion(bf16[2,256,2,256,1]{3,1,2,0,4:T(8,128)(2,1)} %get-tuple-element.89, bf16[1,256,2,256]{3,1,2,0:T(8,128)(2,1)S(1)} %get-tuple-element.80, bf16[1,256,2,256]{3,1,2,0:T(8,128)(2,1)} %copy-done.5, f32[2,256,4,256,1]{3,1,4,2,0:T(8,128)} %get-tuple-element.88, f32[4,256,256]{1,2,0:T(8,128)} %bitcast.218), kind=kOutput, calls=%fused_computation.49 | convolution fusion | flops 1076363264 | bytes 6291456 | tf_op jit(solution)/shard_map/btrc,tcsq->bsrq/dot_general | solution.py:65
  58.6 2.7 %add_reduce_fusion = (bf16[2,256,256]{1,2,0:T(8,128)(2,1)S(1)}, bf16[2,256,256]{1,2,0:T(8,128)(2,1)}, f32[2,256,256]{1,2,0:T(8,128)S(1)}, f32[2,256,256]{1,2,0:T(8,128)S(1)}) fusion(f32[2,2,2,256,256]{3,4,1,0,2:T(8,128)S(1)} %bitcast.212, f32[2,256,256]{1,2,0:T(8,128)} %copy-done.4, f32[2,256,256]{1,2,0:T(8,128)} %copy-done.3, ...), kind=kLoop, calls=%fused_computation.64 | loop fusion | flops 3670016 | bytes 5767168 | tf_op jit(solution)/shard_map/reduce_sum | solution.py:105
  61.4 3.1 %broadcast_in_dim.40 = f32[2,2,640,640]{3,2,1,0:T(8,128)} broadcast(f32[]{:T(128)} %constant.70.clone.1), dimensions={} | broadcast | bytes 6553604 | tf_op jit(solution)/shard_map/vmap(vmap())/broadcast_in_dim;vmap()/broadcast_in_dim | solution.py:133
  64.5 33.3 %while.3 = (s32[]{:T(128)}, f32[2,2,640,640]{3,2,1,0:T(8,128)}, s32[2,4]{1,0:T(2,128)S(1)}, f32[2,2,256,256]{2,3,0,1:T(8,128)S(1)}, s32[]{:T(128)}, /*index=5*/s32[4]{0:T(128)S(1)}, s32[]{:T(128)}) while((s32[]{:T(128)}, f32[2,2,640,640]{3,2,1,0:T(8,128)}, s32[2,4]{1,0:T(2,128)S(1)}, f32[2,2,256,256]{2,3,0,1:T(8,128)S(1)}, s32[]{:T(128)}, ...), condition=%wide.while_cond.1, body=%wide.while_body.1.sunk | while | flops 131101 | bytes 4718791 | solution.py:133
  65.2 3.3 %and_reduce_fusion.2 = pred[]{:T(512)} fusion(s32[4]{0:T(128)S(1)} %get-tuple-element.187, s32[1]{0:T(128)} %bitcast.208, s32[1]{0:T(128)} %bitcast.209, s32[1]{0:T(128)} %bitcast.210, s32[1]{0:T(128)} %bitcast.211), kind=kLoop, calls=%fused_computation.4.clone.1 | loop fusion | flops 27 | bytes 33 | tf_op jit(solution)/shard_map/vmap(vmap())/scatter
  68.7 3.9 %dynamic-slice_select_fusion.2 = f32[1,2,256,256]{3,2,1,0:T(8,128)S(1)} fusion(f32[1,2,256,256]{3,2,1,0:T(8,128)S(1)} %copy.105, f32[2,2,640,640]{3,2,1,0:T(8,128)} %get-tuple-element.176, s32[]{:T(128)} %bitcast.205, s32[]{:T(128)} %bitcast.206, s32[]{:T(128)} %bitcast.207, pred[]{:T(512)} %and_reduce_fusion.2), kind=kLoop, calls=%fused_computation.3.clone.1 | loop fusion | flops 131072 | bytes 1572877 | tf_op jit(solution)/shard_map/vmap(vmap())/scatter
  72.6 8.7 %dynamic-update-slice.8 = f32[2,2,640,640]{3,2,1,0:T(8,128)} dynamic-update-slice(f32[2,2,640,640]{3,2,1,0:T(8,128)} %get-tuple-element.176, f32[1,2,256,256]{3,2,1,0:T(8,128)S(1)} %dynamic-slice_select_fusion.2, s32[]{:T(128)} %bitcast.205, s32[]{:T(128)} %constant.71.clone.1..sunk, s32[]{:T(128)} %bitcast.206, s32[]{:T(128)} %bitcast.207) | dynamic-update-slice | bytes 1048580 | tf_op jit(solution)/shard_map/vmap(vmap())/scatter
  82.0 3.3 %and_reduce_fusion.2 = pred[]{:T(512)} fusion(s32[4]{0:T(128)S(1)} %get-tuple-element.187, s32[1]{0:T(128)} %bitcast.208, s32[1]{0:T(128)} %bitcast.209, s32[1]{0:T(128)} %bitcast.210, s32[1]{0:T(128)} %bitcast.211), kind=kLoop, calls=%fused_computation.4.clone.1 | loop fusion | flops 27 | bytes 33 | tf_op jit(solution)/shard_map/vmap(vmap())/scatter
  85.5 3.9 %dynamic-slice_select_fusion.2 = f32[1,2,256,256]{3,2,1,0:T(8,128)S(1)} fusion(f32[1,2,256,256]{3,2,1,0:T(8,128)S(1)} %copy.105, f32[2,2,640,640]{3,2,1,0:T(8,128)} %get-tuple-element.176, s32[]{:T(128)} %bitcast.205, s32[]{:T(128)} %bitcast.206, s32[]{:T(128)} %bitcast.207, pred[]{:T(512)} %and_reduce_fusion.2), kind=kLoop, calls=%fused_computation.3.clone.1 | loop fusion | flops 131072 | bytes 1572877 | tf_op jit(solution)/shard_map/vmap(vmap())/scatter
  89.4 8.4 %dynamic-update-slice.8 = f32[2,2,640,640]{3,2,1,0:T(8,128)} dynamic-update-slice(f32[2,2,640,640]{3,2,1,0:T(8,128)} %get-tuple-element.176, f32[1,2,256,256]{3,2,1,0:T(8,128)S(1)} %dynamic-slice_select_fusion.2, s32[]{:T(128)} %bitcast.205, s32[]{:T(128)} %constant.71.clone.1..sunk, s32[]{:T(128)} %bitcast.206, s32[]{:T(128)} %bitcast.207) | dynamic-update-slice | bytes 1048580 | tf_op jit(solution)/shard_map/vmap(vmap())/scatter
  97.9 3.8 %reduce_sum.66 = bf16[2,640,640]{2,1,0:T(8,128)(2,1)S(1)} reduce(f32[2,2,640,640]{3,2,1,0:T(8,128)} %get-tuple-element.16, f32[]{:T(128)} %constant.70.clone.1), dimensions={0}, to_apply=%region_5.6 | reduce | flops 819200 | bytes 8192004 | tf_op jit(solution)/shard_map/reduce_sum | solution.py:135
  101.7 5.6 %collective-permute-start.4 = (bf16[2,64,640]{2,1,0:T(8,128)(2,1)S(1)}, bf16[2,64,640]{2,1,0:T(8,128)(2,1)S(1)}, u32[]{:S(2)}, u32[]{:S(2)}) collective-permute-start(bf16[2,64,640]{2,1,0:T(8,128)(2,1)S(1)} %get-tuple-element.69), channel_id=1, source_target_pairs={{0,2},{1,3},{4,6},{5,7},{8,10},{9,11},{12,14},{13,15},{16,18},{17,... | collective-permute-start | bytes 491528 | tf_op jit(solution)/shard_map/ppermute | solution.py:22
  109.5 5.3 %collective-permute-done.5 = bf16[2,64,640]{2,1,0:T(8,128)(2,1)S(1)} collective-permute-done((bf16[2,64,640]{2,1,0:T(8,128)(2,1)S(1)}, bf16[2,64,640]{2,1,0:T(8,128)(2,1)S(1)}, u32[]{:S(2)}, u32[]{:S(2)}) %collective-permute-start.5) | collective-permute-done | bytes 163872 | tf_op jit(solution)/shard_map/ppermute | solution.py:24
  117.7 3.4 %collective-permute-done.6 = bf16[2,768,64]{2,1,0:T(8,128)(2,1)S(1)} collective-permute-done((bf16[2,768,64]{2,1,0:T(8,128)(2,1)S(1)}, bf16[2,768,64]{2,1,0:T(8,128)(2,1)S(1)}, u32[]{:S(2)}, u32[]{:S(2)}) %collective-permute-start.6) | collective-permute-done | bytes 196640 | tf_op jit(solution)/shard_map/ppermute | solution.py:22
  121.1 3.8 %collective-permute-done.7 = bf16[2,768,64]{2,1,0:T(8,128)(2,1)S(1)} collective-permute-done((bf16[2,768,64]{2,1,0:T(8,128)(2,1)S(1)}, bf16[2,768,64]{2,1,0:T(8,128)(2,1)S(1)}, u32[]{:S(2)}, u32[]{:S(2)}) %collective-permute-start.7) | collective-permute-done | bytes 196640 | tf_op jit(solution)/shard_map/ppermute | solution.py:24
  125.1 2.0 maximum_convert_fusion
  127.7 1.8 convert_bitcast_fusion
  129.4 2.1 copy.59
  131.5 18.1 %all-to-all-start = ((bf16[1,2,512,512]{3,1,0,2:T(2,128)(2,1)}), bf16[1,2,512,512]{3,1,0,2:T(2,128)(2,1)S(1)}, u32[]{:S(2)}, u32[]{:S(2)}) async-start(bf16[1,2,512,512]{3,1,0,2:T(2,128)(2,1)} %copy.59), calls=%async_computation | async-start | bytes 2097152 | tf_op jit(solution)/shard_map/all_to_all | solution.py:151
  150.7 48.7 %all-reduce.4.cloned.1.call-done = bf16[2,2,256,256]{2,3,0,1:T(8,128)(2,1)} async-done(((bf16[2,2,256,256]{2,3,0,1:T(8,128)(2,1)}), bf16[2,2,256,256]{2,3,0,1:T(8,128)(2,1)}) %all-reduce.4.cloned.1.call-update) | async-done | bytes 524304 | tf_op jit(solution)/shard_map/psum | solution.py:141
  202.3 4.6 %bitcast_convert_fusion = bf16[64,2,4,1024]{3,0,2,1:T(8,128)(2,1)S(1)} fusion(s32[2,512]{1,0:T(2,128)S(1)} %multiply_add_fusion, bf16[64,2,2,4,512]{4,3,2,1,0:T(4,128)(2,1)S(1)} %bitcast.222), kind=kOutput, calls=%fused_computation.33 | convolution fusion | flops 1097334784 | bytes 2101248 | tf_op jit(solution)/shard_map/ascrt,stv->acrv/dot_general | solution.py:153
  209.5 2.9 %fusion.30 = f32[4,2,8,128]{3,0,1,2:T(4,128)S(1)} fusion(bf16[8,16,2,4,128]{4,3,2,1,0:T(4,128)(2,1)S(1)} %bitcast.221, bf16[8,16,128,128]{3,2,1,0:T(8,128)(2,1)} %param.11), kind=kOutput, calls=%fused_computation.48 | convolution fusion | flops 33554432 | bytes 4489216 | tf_op jit(solution)/shard_map/bkcru,bkuv->rcbv/dot_general | solution.py:159
  (96 shorter events, 34.8 us)
Async XLA Ops:
  7.2 15.4 %copy-start = (bf16[1,2,512,512]{3,2,1,0:T(8,128)(2,1)S(1)}, bf16[1,2,512,512]{3,2,1,0:T(8,128)(2,1)}, u32[]{:S(2)}) copy-start(bf16[1,2,512,512]{3,2,1,0:T(8,128)(2,1)} %param.6) | copy-start | bytes 3145732
  8.3 13.6 %collective-permute-start = (bf16[2,64,512]{2,1,0:T(8,128)(2,1)S(1)}, bf16[2,64,512]{2,1,0:T(8,128)(2,1)S(1)}, u32[]{:S(2)}, u32[]{:S(2)}) collective-permute-start(bf16[2,64,512]{2,1,0:T(8,128)(2,1)S(1)} %get-tuple-element.75), channel_id=1, source_target_pairs={{0,2},{1,3},{4,6},{5,7},{8,10},{9,11},{12,14},{13,15},{16,18},{17,... | collective-permute-start | bytes 393224 | tf_op jit(solution)/shard_map/ppermute | solution.py:22
  13.9 7.9 %collective-permute-start.1 = (bf16[2,64,512]{2,1,0:T(8,128)(2,1)S(1)}, bf16[2,64,512]{2,1,0:T(8,128)(2,1)S(1)}, u32[]{:S(2)}, u32[]{:S(2)}) collective-permute-start(bf16[2,64,512]{2,1,0:T(8,128)(2,1)S(1)} %get-tuple-element.76), channel_id=1, source_target_pairs={{2,0},{3,1},{6,4},{7,5},{10,8},{11,9},{14,12},{15,13},{18,16},{19,... | collective-permute-start | bytes 393224 | tf_op jit(solution)/shard_map/ppermute | solution.py:24
  21.8 11.3 %copy-start.5 = (bf16[1,256,2,256]{3,1,2,0:T(8,128)(2,1)}, bf16[1,256,2,256]{3,1,2,0:T(8,128)(2,1)S(1)}, u32[]{:S(2)}) copy-start(bf16[1,256,2,256]{3,1,2,0:T(8,128)(2,1)S(1)} %get-tuple-element.83) | copy-start | bytes 786436
  21.8 11.3 %copy-start.8 = (bf16[1,256,2,256]{3,1,2,0:T(8,128)(2,1)}, bf16[1,256,2,256]{3,1,2,0:T(8,128)(2,1)S(1)}, u32[]{:S(2)}) copy-start(bf16[1,256,2,256]{3,1,2,0:T(8,128)(2,1)S(1)} %get-tuple-element.79) | copy-start | bytes 786436
  21.8 0.7 copy-start.11
  22.5 1.0 copy-start.12
  23.5 9.6 %collective-permute-start.2 = (bf16[2,640,64]{2,1,0:T(8,128)(2,1)}, bf16[2,640,64]{2,1,0:T(8,128)(2,1)}, u32[]{:S(2)}, u32[]{:S(2)}) collective-permute-start(bf16[2,640,64]{2,1,0:T(8,128)(2,1)} %get-tuple-element.71), channel_id=1, source_target_pairs={{0,1},{2,3},{4,5},{6,7},{8,9},{10,11},{12,13},{14,15},{16,17},{18,... | collective-permute-start | bytes 491528 | tf_op jit(solution)/shard_map/ppermute | solution.py:22
  26.5 10.2 %collective-permute-start.3 = (bf16[2,640,64]{2,1,0:T(8,128)(2,1)}, bf16[2,640,64]{2,1,0:T(8,128)(2,1)}, u32[]{:S(2)}, u32[]{:S(2)}) collective-permute-start(bf16[2,640,64]{2,1,0:T(8,128)(2,1)} %get-tuple-element.72), channel_id=1, source_target_pairs={{1,0},{3,2},{5,4},{7,6},{9,8},{11,10},{13,12},{15,14},{17,16},{19,... | collective-permute-start | bytes 491528 | tf_op jit(solution)/shard_map/ppermute | solution.py:24
  38.9 7.4 %copy-start.1 = (f32[2,256,256]{1,2,0:T(8,128)S(1)}, f32[2,256,256]{1,2,0:T(8,128)}, u32[]{:S(2)}) copy-start(f32[2,256,256]{1,2,0:T(8,128)} %copy.50) | copy-start | bytes 1572868
  44.8 2.9 %copy-start.9 = (bf16[1,256,2,256]{3,1,2,0:T(8,128)(2,1)S(1)}, bf16[1,256,2,256]{3,1,2,0:T(8,128)(2,1)}, u32[]{:S(2)}) copy-start(bf16[1,256,2,256]{3,1,2,0:T(8,128)(2,1)} %copy-done.8) | copy-start | bytes 786436
  44.8 2.9 %copy-start.10 = (bf16[1,256,2,256]{3,1,2,0:T(8,128)(2,1)S(1)}, bf16[1,256,2,256]{3,1,2,0:T(8,128)(2,1)}, u32[]{:S(2)}) copy-start(bf16[1,256,2,256]{3,1,2,0:T(8,128)(2,1)} %get-tuple-element.84) | copy-start | bytes 786436
  46.2 6.5 %copy-start.3 = (f32[2,256,256]{1,2,0:T(8,128)}, f32[2,256,256]{1,2,0:T(8,128)S(1)}, u32[]{:S(2)}) copy-start(f32[2,256,256]{1,2,0:T(8,128)S(1)} %copy.49) | copy-start | bytes 1572868
  46.4 6.3 %copy-start.4 = (f32[2,256,256]{1,2,0:T(8,128)}, f32[2,256,256]{1,2,0:T(8,128)S(1)}, u32[]{:S(2)}) copy-start(f32[2,256,256]{1,2,0:T(8,128)S(1)} %copy.51) | copy-start | bytes 1572868
  47.7 6.4 %copy-start.6 = (bf16[1,1,1,2,256,256]{4,5,3,2,1,0:T(8,128)(2,1)S(1)}, bf16[1,1,1,2,256,256]{4,5,3,2,1,0:T(8,128)(2,1)}, u32[]{:S(2)}) copy-start(bf16[1,1,1,2,256,256]{4,5,3,2,1,0:T(8,128)(2,1)} %copy.54) | copy-start | bytes 786436
  55.2 3.4 %copy-start.2 = (f32[2,256,256]{1,2,0:T(8,128)S(1)}, f32[2,256,256]{1,2,0:T(8,128)}, u32[]{:S(2)}) copy-start(f32[2,256,256]{1,2,0:T(8,128)} %copy.50) | copy-start | bytes 1572868
  61.4 3.2 %copy-start.13 = (s32[4]{0:T(128)S(1)}, s32[4]{0:T(128)}, u32[]{:S(2)}) copy-start(s32[4]{0:T(128)} %constant.300) | copy-start | bytes 52
  101.7 7.9 %collective-permute-start.4 = (bf16[2,64,640]{2,1,0:T(8,128)(2,1)S(1)}, bf16[2,64,640]{2,1,0:T(8,128)(2,1)S(1)}, u32[]{:S(2)}, u32[]{:S(2)}) collective-permute-start(bf16[2,64,640]{2,1,0:T(8,128)(2,1)S(1)} %get-tuple-element.69), channel_id=1, source_target_pairs={{0,2},{1,3},{4,6},{5,7},{8,10},{9,11},{12,14},{13,15},{16,18},{17,... | collective-permute-start | bytes 491528 | tf_op jit(solution)/shard_map/ppermute | solution.py:22
  107.3 7.6 %collective-permute-start.5 = (bf16[2,64,640]{2,1,0:T(8,128)(2,1)S(1)}, bf16[2,64,640]{2,1,0:T(8,128)(2,1)S(1)}, u32[]{:S(2)}, u32[]{:S(2)}) collective-permute-start(bf16[2,64,640]{2,1,0:T(8,128)(2,1)S(1)} %get-tuple-element.70), channel_id=1, source_target_pairs={{2,0},{3,1},{6,4},{7,5},{10,8},{11,9},{14,12},{15,13},{18,16},{19,... | collective-permute-start | bytes 491528 | tf_op jit(solution)/shard_map/ppermute | solution.py:24
  115.1 6.0 %collective-permute-start.6 = (bf16[2,768,64]{2,1,0:T(8,128)(2,1)S(1)}, bf16[2,768,64]{2,1,0:T(8,128)(2,1)S(1)}, u32[]{:S(2)}, u32[]{:S(2)}) collective-permute-start(bf16[2,768,64]{2,1,0:T(8,128)(2,1)S(1)} %get-tuple-element.67), channel_id=1, source_target_pairs={{0,1},{2,3},{4,5},{6,7},{8,9},{10,11},{12,13},{14,15},{16,17},{18,... | collective-permute-start | bytes 589832 | tf_op jit(solution)/shard_map/ppermute | solution.py:22
  116.4 8.5 %collective-permute-start.7 = (bf16[2,768,64]{2,1,0:T(8,128)(2,1)S(1)}, bf16[2,768,64]{2,1,0:T(8,128)(2,1)S(1)}, u32[]{:S(2)}, u32[]{:S(2)}) collective-permute-start(bf16[2,768,64]{2,1,0:T(8,128)(2,1)S(1)} %get-tuple-element.68), channel_id=1, source_target_pairs={{1,0},{3,2},{5,4},{7,6},{9,8},{11,10},{13,12},{15,14},{17,16},{19,... | collective-permute-start | bytes 589832 | tf_op jit(solution)/shard_map/ppermute | solution.py:24
  125.0 2.0 copy-start.15
  129.4 20.3 %copy-start.7 = (bf16[2,256,256]{1,2,0:T(8,128)(2,1)S(1)}, bf16[2,256,256]{1,2,0:T(8,128)(2,1)}, u32[]{:S(2)}) copy-start(bf16[2,256,256]{1,2,0:T(8,128)(2,1)} %get-tuple-element.34) | copy-start | bytes 786436
  129.4 21.1 %copy-start.14 = (s32[8,16]{1,0:T(8,128)S(1)}, s32[8,16]{1,0:T(8,128)}, u32[]{:S(2)}) copy-start(s32[8,16]{1,0:T(8,128)} %param.10) | copy-start | bytes 1540
  131.5 70.3 %all-to-all-start = ((bf16[1,2,512,512]{3,1,0,2:T(2,128)(2,1)}), bf16[1,2,512,512]{3,1,0,2:T(2,128)(2,1)S(1)}, u32[]{:S(2)}, u32[]{:S(2)}) async-start(bf16[1,2,512,512]{3,1,0,2:T(2,128)(2,1)} %copy.59), calls=%async_computation | async-start | bytes 2097152 | tf_op jit(solution)/shard_map/all_to_all | solution.py:151
  149.6 49.8 %all-reduce.4.cloned.1.call-start = ((), (), s32[]{:S(2)}) async-start(), calls=%async_computation.1 | async-start | bytes 1048576 | tf_op jit(solution)/shard_map/psum | solution.py:141
Sparse Core Ops, SparseCore 0:
  153.4 45.9 all-reduce.3
where the time goes:
time: 223 us; the launch traced here: 220 us
  waiting for transfers between devices  65.8 us (30%)
  local copies, waits for them, and re-layouts  42.7 us (19%)
  other arithmetic  41.9 us (19%)
  starting transfers between devices  39.1 us (18%)
  matrix products  16 us (7%)
  between operations  14.4 us (6%)
    psum x1, waiting for transfers between devices, body(): lax.psum(probe_part.astype(jnp.bfloat16), ('sy', 'sx')).astype(jnp.float32)  48.7 us
    scatter x10, local copies, waits for them, and re-layouts  18.9 us
    all_to_all x1, starting transfers between devices, body(): lax.all_to_all(sinogram, ('ang', 'sx'), split_axis=2, concat_axis=0, tile...  18.1 us
    ppermute x4, starting transfers between devices, with_halo(): lax.ppermute(tail, axis, [(i, (i + 1) % count) for i in range(ends)])  15.6 us
    scatter x4, other arithmetic  14.4 us
    ppermute x4, waiting for transfers between devices, with_halo(): lax.ppermute(head, axis, [((i + 1) % count, i) for i in range(ends)])  12.8 us
    dot_general x2, matrix products, right_product(): jnp.einsum('btrc,tcsq->bsrq', fields, matrix, preferred_element_type=jnp....  8.42 us
    gather x6, local copies, waits for them, and re-layouts  5.79 us
  transfers between devices with their start and end apart: 10, of which 6 were waited for; matrix products, arithmetic and copies ran while one was open for 7% of the time, Pallas kernels for 0%

commit v1 on v0

v1 whole, which is shorter than its diff:
```python
import functools
import math

import jax
import jax.numpy as jnp
import numpy as np
from jax import lax
from jax.experimental import pallas as pl
from jax.experimental.pallas import tpu as pltpu
from jax.sharding import PartitionSpec as P

PATCH = 256
RIM = 64
BLK = 128
TILE = 512
ROWS = 640
COLS = 768
MESH = pl.DeviceIdType.MESH
BF = jnp.bfloat16
F32 = jnp.float32


def dft_tables():
    ids = np.arange(PATCH)
    phases = (np.outer(ids, ids) % PATCH).astype(np.float64) * (2.0 * math.pi / PATCH)
    factor = 1.0 / math.sqrt(PATCH)
    real = (np.cos(phases) * factor).astype(np.float32)
    imag = (-np.sin(phases) * factor).astype(np.float32)
    forward = np.block([[real, -imag], [imag, real]])
    backward = np.block([[real, imag], [-imag, real]])
    return forward.astype(BF), backward.astype(BF)


def ramp_blocks(line_blocks):
    x = np.arange((2 * line_blocks - 1) * BLK)
    n = np.arange(BLK)[None, :] - (x - (line_blocks - 1) * BLK)[:, None]
    odd = n % 2 != 0
    scaled = n.astype(np.float32) * np.float32(math.pi)
    values = np.where(odd, -1.0 / np.maximum(scaled * scaled, 1.0), 0.0)
    values = np.where(n == 0, 0.25, values).astype(np.float32)
    return values.astype(BF)


def strips_kernel(obj_ref, row_out, col_out, cor_out, send_sem, recv_sem):
    ang, sy, sx = lax.axis_index("ang"), lax.axis_index("sy"), lax.axis_index("sx")
    oy, ox = 1 - sy, 1 - sx
    devices = [(ang, oy, sx), (ang, sy, ox), (ang, oy, ox)]
    barrier = pltpu.get_barrier_semaphore()
    for dev in devices:
        pl.semaphore_signal(barrier, inc=1, device_id=dev, device_id_type=MESH)
    pl.semaphore_wait(barrier, 3)
    rows = pl.ds(pl.multiple_of((TILE - RIM) * oy, RIM), RIM)
    cols = pl.ds(pl.multiple_of((TILE - BLK) * ox, BLK), BLK)
    sources = [obj_ref.at[0, :, rows, :], obj_ref.at[0, :, :, cols], obj_ref.at[0, :, rows, cols]]
    copies = [
        pltpu.make_async_remote_copy(
            src_ref=src, dst_ref=dst, send_sem=send_sem.at[i], recv_sem=recv_sem.at[i],
            device_id=dev, device_id_type=MESH,
        )
        for i, (src, dst, dev) in enumerate(zip(sources, (row_out, col_out, cor_out), devices))
    ]
    for copy in copies:
        copy.start()
    for copy in copies:
        copy.wait()


def patch_kernel(
    angles,
    pos_ref, bi_ref,
    obj_ref, halo_row, halo_col, halo_cor, probe_ref, data_ref, fwd_ref, bwd_ref, ramp_ref, bv_ref,
    og_out, row_out, col_out, cor_out, part_out, ramp_out, bv_out,
    big, probe, data, fwd, bwd, ramp, bv,
    win, patch, exits, half, far, chi, placed, og,
    rim_row, rim_col, rim_cor, part,
    load_sem, pick_sem, out_sem,
):
    ang, sy, sx = lax.axis_index("ang"), lax.axis_index("sy"), lax.axis_index("sx")
    oy, ox = 1 - sy, 1 - sx
    dst_row = pl.ds(pl.multiple_of((ROWS - RIM) * oy, RIM), RIM)
    dst_col = pl.ds(pl.multiple_of((COLS - BLK) * ox, BLK), BLK)
    loads = [
        pltpu.make_async_copy(src, dst, load_sem.at[i])
        for i, (src, dst) in enumerate(
            [
                (obj_ref.at[0], big.at[:, pl.ds(RIM, TILE), pl.ds(BLK, TILE)]),
                (halo_row, big.at[:, dst_row, pl.ds(BLK, TILE)]),
                (halo_col, big.at[:, pl.ds(RIM, TILE), dst_col]),
                (halo_cor, big.at[:, dst_row, dst_col]),
                (probe_ref, probe),
                (fwd_ref, fwd),
                (bwd_ref, bwd),
                (data_ref.at[0, 0, 0], data),
            ]
        )
    ]
    for copy in loads:
        copy.start()

    big[:, pl.ds(pl.multiple_of((ROWS - RIM) * sy, RIM), RIM), :] = jnp.zeros((2, RIM, COLS), BF)
    big[:, :, pl.ds(pl.multiple_of((COLS - BLK) * sx, BLK), BLK)] = jnp.zeros((2, ROWS, BLK), BF)
    for q in range(4):
        placed[q, :, 0:RIM, :] = jnp.zeros((5, RIM, BLK), F32)
        placed[q, :, RIM + PATCH :, :] = jnp.zeros((5, RIM, BLK), F32)
        placed[q, 0, RIM : RIM + PATCH, :] = jnp.zeros((PATCH, BLK), F32)
        placed[q, 4, RIM : RIM + PATCH, :] = jnp.zeros((PATCH, BLK), F32)

    named = [(jnp.int32(-1), jnp.int32(0)), (jnp.int32(0), jnp.int32(0))]
    for j in range(2 * angles):
        entry = bi_ref[j // 16, j % 16]
        mine = (entry >> 3) == ang
        early = jnp.logical_and(mine, named[0][0] < 0)
        named = [
            (jnp.where(take, j, at), jnp.where(take, entry & 7, column))
            for take, (at, column) in zip((early, mine), named)
        ]
    named[0] = (jnp.maximum(named[0][0], 0), named[0][1])
    picks = []
    for s, (entry, column) in enumerate(named):
        at = pl.multiple_of((7 - column + 4 * sx) * BLK, BLK)
        picks.append(
            pltpu.make_async_copy(ramp_ref.at[pl.ds(at, TILE), :], ramp.at[s], pick_sem.at[2 * s])
        )
        picks.append(
            pltpu.make_async_copy(bv_ref.at[entry >> 4, entry & 15], bv.at[s], pick_sem.at[2 * s + 1])
        )
    for copy in picks:
        copy.start()
    for copy in loads:
        copy.wait()

    def corner(p):
        return pos_ref[0, 0, 0, p, 0], pos_ref[0, 0, 0, p, 1] + RIM

    def forward_patch(p, carry):
        u, v = corner(p)
        base = jnp.minimum(u >> 4, 23) * 16
        lead = u - base
        block, shift = v >> 7, v & (BLK - 1)
        across = lax.broadcasted_iota(jnp.int32, (384, PATCH), 0)
        pick = jnp.where(
            across == lax.broadcasted_iota(jnp.int32, (384, PATCH), 1) + shift, 1.0, 0.0
        ).astype(BF)
        for c in range(2):
            cells = big[
                c, pl.ds(pl.multiple_of(base, 16), 272), pl.ds(pl.multiple_of(block * BLK, BLK), 384)
            ]
            cells = jnp.dot(cells, pick, preferred_element_type=F32)
            for b in range(2):
                win[c, b] = cells[:, b * BLK : (b + 1) * BLK]
        for c in range(2):
            for b in range(2):
                patch[p, c, :, b * BLK : (b + 1) * BLK] = win[c, b, pl.ds(lead, PATCH), :]
        for m in range(2):
            exits[m, 0:PATCH] = (probe[m, 0] * patch[p, 0] - probe[m, 1] * patch[p, 1]).astype(BF)
            exits[m, PATCH:] = (probe[m, 0] * patch[p, 1] + probe[m, 1] * patch[p, 0]).astype(BF)
        for m in range(2):
            done = jnp.dot(fwd[...], exits[m], preferred_element_type=F32)
            half[m, :, 0:PATCH] = done[0:PATCH].astype(BF)
            half[m, :, PATCH:] = done[PATCH:].astype(BF)
        for m in range(2):
            far[m] = jnp.dot(half[m], bwd[...], preferred_element_type=F32)
        misfit = (
            far[0, :, 0:PATCH] * far[0, :, 0:PATCH]
            + far[0, :, PATCH:] * far[0, :, PATCH:]
            + far[1, :, 0:PATCH] * far[1, :, 0:PATCH]
            + far[1, :, PATCH:] * far[1, :, PATCH:]
            - data[p].astype(F32)
        )
        for m in range(2):
            exits[m, 0:PATCH] = (misfit * far[m, :, 0:PATCH]).astype(BF)
            exits[m, PATCH:] = (misfit * far[m, :, PATCH:]).astype(BF)
        for m in range(2):
            done = jnp.dot(bwd[...], exits[m], preferred_element_type=F32)
            half[m, :, 0:PATCH] = done[0:PATCH].astype(BF)
            half[m, :, PATCH:] = done[PATCH:].astype(BF)
        for m in range(2):
            chi[p, m] = jnp.dot(half[m], fwd[...], preferred_element_type=F32)
        cr = [chi[p, m, :, 0:PATCH] for m in range(2)]
        ci = [chi[p, m, :, PATCH:] for m in range(2)]
        grad = [
            probe[0, 0] * cr[0] + probe[0, 1] * ci[0] + probe[1, 0] * cr[1] + probe[1, 1] * ci[1],
            probe[0, 0] * ci[0] - probe[0, 1] * cr[0] + probe[1, 0] * ci[1] - probe[1, 1] * cr[1],
        ]
        spots = lax.broadcasted_iota(jnp.int32, (PATCH, 384), 1)
        put = jnp.where(
            spots == lax.broadcasted_iota(jnp.int32, (PATCH, 384), 0) + shift, 1.0, 0.0
        ).astype(BF)
        for c in range(2):
            high = grad[c].astype(BF)
            low = (grad[c] - high.astype(F32)).astype(BF)
            moved = jnp.dot(high, put, preferred_element_type=F32) + jnp.dot(
                low, put, preferred_element_type=F32
            )
            for b in range(3):
                placed[p * 2 + c, b + 1, RIM : RIM + PATCH, :] = moved[:, b * BLK : (b + 1) * BLK]
        return carry

    lax.fori_loop(0, 2, forward_patch, 0)

    def cells_at(c, row_chunk, lane_block):
        total_cells = None
        for p in range(2):
            u, v = corner(p)
            row = jnp.minimum(jnp.maximum(row_chunk * RIM - u + RIM, 0), PATCH + RIM)
            lane = jnp.minimum(jnp.maximum(lane_block - (v >> 7), -1), 3) + 1
            term = placed[p * 2 + c, lane, pl.ds(row, RIM), :]
            total_cells = term if total_cells is None else total_cells + term
        return total_cells

    rim_chunk = 9 * oy
    rim_block = 5 * ox
    for c in range(2):
        for b in range(4):
            rim_row[c, :, b * BLK : (b + 1) * BLK] = cells_at(c, rim_chunk, b + 1).astype(BF)
        rim_cor[c] = cells_at(c, rim_chunk, rim_block).astype(BF)

    def rim_columns(r, carry):
        for c in range(2):
            rim_col[c, pl.ds(pl.multiple_of(r * RIM, RIM), RIM), :] = cells_at(
                c, r + 1, rim_block
            ).astype(BF)
        return carry

    lax.fori_loop(0, 8, rim_columns, 0)
    outs = [
        pltpu.make_async_copy(src, dst, out_sem.at[i])
        for i, (src, dst) in enumerate(
            [
                (rim_row, row_out), (rim_col, col_out), (rim_cor, cor_out),
                (og, og_out), (part, part_out), (ramp, ramp_out), (bv, bv_out),
            ]
        )
    ]
    for copy in outs[:3]:
        copy.start()
    for copy in picks:
        copy.wait()
    for copy in outs[5:]:
        copy.start()

    def interior(r, carry):
        for c in range(2):
            for b in range(4):
                og[c, pl.ds(pl.multiple_of(r * RIM, RIM), RIM), b * BLK : (b + 1) * BLK] = cells_at(
                    c, r + 1, b + 1
                )
        return carry

    lax.fori_loop(0, 8, interior, 0)

    outs[3].start()

    for m in range(2):
        part[2 * m] = (
            patch[0, 0] * chi[0, m, :, 0:PATCH] + patch[0, 1] * chi[0, m, :, PATCH:]
            + patch[1, 0] * chi[1, m, :, 0:PATCH] + patch[1, 1] * chi[1, m, :, PATCH:]
        ).astype(BF)
        part[2 * m + 1] = (
            patch[0, 0] * chi[0, m, :, PATCH:] - patch[0, 1] * chi[0, m, :, 0:PATCH]
            + patch[1, 0] * chi[1, m, :, PATCH:] - patch[1, 1] * chi[1, m, :, 0:PATCH]
        ).astype(BF)
    outs[4].start()
    for copy in outs:
        copy.wait()


def regroup_kernel(
    angles,
    og_ref, row_ref, col_ref, cor_ref, part_ref, ramp_ref, bv_ref,
    og_out, total_out, inbox_out,
    og, part, ramp, bv, got_row, got_col, got_cor, part_got, total_send, total, sino, msgs, inbox,
    load_sem, rim_send, rim_recv,
    part_ssem, part_rsem, tot_ssem, tot_rsem, a2a_send, a2a_recv, own_sem, out_sem,
):
    ang, sy, sx = lax.axis_index("ang"), lax.axis_index("sy"), lax.axis_index("sx")
    oy, ox = 1 - sy, 1 - sx
    group = 2 * angles
    me = ang * 2 + sx
    tile = sy * 2 + sx

    barrier = pltpu.get_barrier_semaphore()
    for dev in ((ang, oy, sx), (ang, oy, ox)):
        pl.semaphore_signal(barrier, inc=1, device_id=dev, device_id_type=MESH)

    def greet(k, carry):
        d = lax.rem(me + k, group)
        pl.semaphore_signal(
            barrier, inc=1, device_id=(d // 2, sy, lax.rem(d, 2)), device_id_type=MESH
        )
        return carry

    lax.fori_loop(1, group, greet, 0)
    loads = [
        pltpu.make_async_copy(src, dst, load_sem.at[i])
        for i, (src, dst) in enumerate(
            [(og_ref, og), (ramp_ref, ramp), (bv_ref, bv), (part_ref.at[tile], part)]
        )
    ]
    for copy in loads:
        copy.start()
    pl.semaphore_wait(barrier, group + 1)

    rims = [
        pltpu.make_async_remote_copy(
            src_ref=src, dst_ref=dst, send_sem=rim_send.at[i], recv_sem=rim_recv.at[i],
            device_id=dev, device_id_type=MESH,
        )
        for i, (src, dst, dev) in enumerate(
            [
                (row_ref, got_row, (ang, oy, sx)),
                (col_ref, got_col, (ang, sy, ox)),
                (cor_ref, got_cor, (ang, oy, ox)),
            ]
        )
    ]
    for copy in rims:
        copy.start()
    others = [(sy, ox), (oy, sx), (oy, ox)]
    part_copies = [
        pltpu.make_async_remote_copy(
            src_ref=part_ref.at[ty * 2 + tx], dst_ref=part_got.at[i],
            send_sem=part_ssem.at[i], recv_sem=part_rsem.at[i],
            device_id=(ang, ty, tx), device_id_type=MESH,
        )
        for i, (ty, tx) in enumerate(others)
    ]
    for copy in part_copies:
        copy.start()
    for copy in loads:
        copy.wait()
    for copy in rims:
        copy.wait()
    row_at = pl.ds(pl.multiple_of((TILE - RIM) * oy, RIM), RIM)
    col_at = pl.ds(pl.multiple_of((TILE - BLK) * ox, BLK), BLK)
    for c in range(2):
        og[c, row_at, :] = og[c, row_at, :] + got_row[c].astype(F32)
        og[c, :, col_at] = og[c, :, col_at] + got_col[c].astype(F32)
        og[c, row_at, col_at] = og[c, row_at, col_at] + got_cor[c].astype(F32)
    og_copy = pltpu.make_async_copy(og, og_out, out_sem.at[0])
    og_copy.start()

    sino[...] = og[...].astype(BF).reshape(2 * TILE, TILE)
    lines = []
    for s in range(2):
        filtered = jnp.dot(sino[...], ramp[s], preferred_element_type=F32).astype(BF)
        lines.append(jnp.dot(filtered, bv[s], preferred_element_type=F32))
    top = lax.broadcasted_iota(jnp.int32, (64, 8, BLK), 1) < 4
    for s in range(2):
        a = lines[s][0:TILE].reshape(64, 8, BLK)
        b = lines[s][TILE:].reshape(64, 8, BLK)
        lanes = slice(s * BLK, (s + 1) * BLK)
        msgs[:, 0, :, lanes] = jnp.where(top, a, pltpu.roll(b, 4, 1)).astype(BF)
        msgs[:, 1, :, lanes] = jnp.where(top, pltpu.roll(a, 4, 1), b).astype(BF)

    def send(k, carry):
        d = lax.rem(me + k, group)
        pltpu.make_async_remote_copy(
            src_ref=msgs.at[d // 2, lax.rem(d, 2)], dst_ref=inbox.at[me],
            send_sem=a2a_send, recv_sem=a2a_recv,
            device_id=(d // 2, sy, lax.rem(d, 2)), device_id_type=MESH,
        ).start()
        return carry

    lax.fori_loop(1, group, send, 0)
    own = pltpu.make_async_copy(msgs.at[ang, sx], inbox.at[me], own_sem)
    own.start()

    for copy in part_copies:
        copy.wait()
    summed = part[...].astype(F32) + part_got[0].astype(F32) + part_got[1].astype(F32) + part_got[2].astype(F32)
    total_send[...] = summed.astype(BF)
    total[tile] = total_send[...]
    total_copies = [
        pltpu.make_async_remote_copy(
            src_ref=total_send, dst_ref=total.at[tile],
            send_sem=tot_ssem.at[i], recv_sem=tot_rsem.at[i],
            device_id=(ang, ty, tx), device_id_type=MESH,
        )
        for i, (ty, tx) in enumerate(others)
    ]
    for copy in total_copies:
        copy.start()

    own.wait()
    pltpu.make_async_copy(
        inbox.at[pl.ds(0, group - 1)], inbox.at[pl.ds(0, group - 1)], a2a_recv
    ).wait()
    inbox_copy = pltpu.make_async_copy(inbox, inbox_out, out_sem.at[1])
    inbox_copy.start()
    for copy in total_copies:
        copy.wait()
    total_copy = pltpu.make_async_copy(total, total_out, out_sem.at[2])
    total_copy.start()
    pltpu.make_async_copy(
        inbox.at[pl.ds(0, group - 1)], inbox.at[pl.ds(0, group - 1)], a2a_send
    ).wait()
    og_copy.wait()
    inbox_copy.wait()
    total_copy.wait()


def finish_kernel(
    angles, bi_ref, og_ref, total_ref, inbox_ref, og_out, pg_out, vol_out,
    og, total, pg, inbox, vol, seen, in_sem, og_sem, out_sem,
):
    arrived = pltpu.make_async_copy(inbox_ref, inbox, in_sem.at[0])
    summed = pltpu.make_async_copy(total_ref, total, in_sem.at[1])
    arrived.start()
    summed.start()
    pieces = [
        (
            pltpu.make_async_copy(og_ref.at[:, pl.ds(i * 128, 128)], og.at[:, pl.ds(i * 128, 128)], og_sem.at[i]),
            pltpu.make_async_copy(og.at[:, pl.ds(i * 128, 128)], og_out.at[0, :, pl.ds(i * 128, 128)], og_sem.at[i + 4]),
        )
        for i in range(4)
    ]
    for load, _ in pieces:
        load.start()
    for a in range(angles):
        seen[a] = 0
    summed.wait()
    for q in range(4):
        pg[0, q // 2, q % 2] = total[q].astype(F32) * (1.0 / math.sqrt(8.0))
    pg_copy = pltpu.make_async_copy(pg, pg_out, out_sem.at[0])
    pg_copy.start()
    for load, store in pieces:
        load.wait()
        store.start()
    arrived.wait()
    for b in range(8):
        line = jnp.zeros((8, BLK), F32)
        for k in range(16):
            source = bi_ref[b, k] >> 3
            slot = seen[source]
            seen[source] = 1
            lane = pl.multiple_of(slot * BLK, BLK)
            for h in range(2):
                line = line + inbox[source * 2 + h, :, pl.ds(lane, BLK)].astype(F32)
        for c in range(2):
            for r in range(4):
                vol[0, r, c, b * BLK : (b + 1) * BLK] = line[c * 4 + r]
    vol_copy = pltpu.make_async_copy(vol, vol_out, out_sem.at[1])
    vol_copy.start()
    for _, store in pieces:
        store.wait()
    pg_copy.wait()
    vol_copy.wait()


def body(angles, tables, objects, probe, data, positions, block_index, block_values):
    forward, backward, ramp = (jnp.asarray(t) for t in tables)
    group = 2 * angles
    dma = pltpu.SemaphoreType.DMA
    smem = pl.BlockSpec(memory_space=pltpu.SMEM)
    hbm = pl.BlockSpec(memory_space=pl.ANY)

    def shape(dims, kind):
        return jax.ShapeDtypeStruct(dims, kind)

    rim_shapes = (shape((2, RIM, TILE), BF), shape((2, TILE, BLK), BF), shape((2, RIM, BLK), BF))
    halos = pl.pallas_call(
        strips_kernel,
        out_shape=rim_shapes,
        in_specs=[hbm],
        out_specs=[hbm] * 3,
        scratch_shapes=[dma((3,)), dma((3,))],
        compiler_params=pltpu.CompilerParams(collective_id=0, has_side_effects=True),
    )(objects)
    og_part, row, col, cor, parts, ramp_two, bv_two = pl.pallas_call(
        functools.partial(patch_kernel, angles),
        out_shape=(shape((2, TILE, TILE), F32),) + rim_shapes + (
            shape((4, PATCH, PATCH), BF), shape((2, TILE, BLK), BF), shape((2, BLK, BLK), BF),
        ),
        in_specs=[smem] * 2 + [hbm] * 10,
        out_specs=[hbm] * 7,
        scratch_shapes=[
            pltpu.VMEM((2, ROWS, COLS), BF),
            pltpu.VMEM((2, 2, PATCH, PATCH), F32),
            pltpu.VMEM((2, PATCH, PATCH), BF),
            pltpu.VMEM((512, 512), BF),
            pltpu.VMEM((512, 512), BF),
            pltpu.VMEM((2, TILE, BLK), BF),
            pltpu.VMEM((2, BLK, BLK), BF),
            pltpu.VMEM((2, 2, 272, BLK), F32),
            pltpu.VMEM((2, 2, PATCH, PATCH), F32),
            pltpu.VMEM((2, 512, PATCH), BF),
            pltpu.VMEM((2, PATCH, 512), BF),
            pltpu.VMEM((2, PATCH, 512), F32),
            pltpu.VMEM((2, 2, PATCH, 512), F32),
            pltpu.VMEM((4, 5, 384, BLK), F32),
            pltpu.VMEM((2, TILE, TILE), F32),
            pltpu.VMEM((2, RIM, TILE), BF),
            pltpu.VMEM((2, TILE, BLK), BF),
            pltpu.VMEM((2, RIM, BLK), BF),
            pltpu.VMEM((4, PATCH, PATCH), BF),
            dma((8,)), dma((4,)), dma((7,)),
        ],
        compiler_params=pltpu.CompilerParams(vmem_limit_bytes=40 * 1024 * 1024),
    )(positions, block_index, objects, *halos, probe, data, forward, backward, ramp, block_values)
    og, total, inbox = pl.pallas_call(
        functools.partial(regroup_kernel, angles),
        out_shape=(
            shape((2, TILE, TILE), F32), shape((4, PATCH, PATCH), BF), shape((group, 8, 2 * BLK), BF),
        ),
        in_specs=[hbm] * 7,
        out_specs=[hbm] * 3,
        scratch_shapes=[
            pltpu.VMEM((2, TILE, TILE), F32),
            pltpu.VMEM((PATCH, PATCH), BF),
            pltpu.VMEM((2, TILE, BLK), BF),
            pltpu.VMEM((2, BLK, BLK), BF),
            pltpu.VMEM((2, RIM, TILE), BF),
            pltpu.VMEM((2, TILE, BLK), BF),
            pltpu.VMEM((2, RIM, BLK), BF),
            pltpu.VMEM((3, PATCH, PATCH), BF),
            pltpu.VMEM((PATCH, PATCH), BF),
            pltpu.VMEM((4, PATCH, PATCH), BF),
            pltpu.VMEM((2 * TILE, TILE), BF),
            pltpu.VMEM((group // 2, 2, 8, 2 * BLK), BF),
            pltpu.VMEM((group, 8, 2 * BLK), BF),
            dma((4,)), dma((3,)), dma((3,)),
            dma((3,)), dma((3,)), dma((3,)), dma((3,)), dma, dma, dma, dma((3,)),
        ],
        compiler_params=pltpu.CompilerParams(
            collective_id=1, has_side_effects=True, vmem_limit_bytes=40 * 1024 * 1024
        ),
    )(og_part, row, col, cor, parts, ramp_two, bv_two)
    return pl.pallas_call(
        functools.partial(finish_kernel, angles),
        out_shape=(
            shape((1, 2, TILE, TILE), F32), shape((1, 2, 2, PATCH, PATCH), F32), shape((1, 4, 2, 1024), F32),
        ),
        in_specs=[smem] + [hbm] * 3,
        out_specs=[hbm] * 3,
        scratch_shapes=[
            pltpu.VMEM((2, TILE, TILE), F32),
            pltpu.VMEM((4, PATCH, PATCH), BF),
            pltpu.VMEM((1, 2, 2, PATCH, PATCH), F32),
            pltpu.VMEM((group, 8, 2 * BLK), BF),
            pltpu.VMEM((1, 4, 2, 1024), F32),
            pltpu.SMEM((angles,), jnp.int32),
            dma((2,)), dma((8,)), dma((2,)),
        ],
        compiler_params=pltpu.CompilerParams(vmem_limit_bytes=40 * 1024 * 1024),
    )(block_index, og, total, inbox)


def solution(mesh):
    tables = dft_tables() + (ramp_blocks(8),)
    return jax.shard_map(
        functools.partial(body, mesh.shape["ang"], tables),
        mesh=mesh,
        in_specs=(
            P("ang", None, "sy", "sx"),
            P(),
            P("ang", "sy", "sx", None, None, None),
            P("ang", "sy", "sx", None, None),
            P(),
            P(),
        ),
        out_specs=(
            P("ang", None, "sy", "sx"),
            P("ang", None, None, None, None),
            P("sy", ("ang", "sx"), None, None),
        ),
        check_vma=False,
    )
```

time: 223 us -> 78.7 us (0.35); the launches traced: 220 us -> 78.2 us
  waiting for transfers between devices: 65.8 us -> 0 us
  Pallas kernels: 0 us -> 64.8 us
  other arithmetic: 41.9 us -> 0 us
  starting transfers between devices: 39.1 us -> 0 us
  local copies, waits for them, and re-layouts: 42.7 us -> 12.7 us
  matrix products: 16 us -> 0 us
  between operations: 14.4 us -> 0.67 us
    pallas_call x0 -> x4, Pallas kernels: none -> 64.8 us  [the longest x1 41 us: body(): pl.pallas_call(functools.partial(regroup_kernel, angles), out_shape=(shap...]
    psum x1 -> x0, waiting for transfers between devices: 48.7 us -> none  [body(): lax.psum(probe_part.astype(jnp.bfloat16), ('sy', 'sx')).astype(jnp.float32)]
    ppermute x8 -> x0, starting transfers between devices: 20.9 us -> none  [the longest x4 15.6 us: with_halo(): lax.ppermute(tail, axis, [(i, (i + 1) % count) for i in range(ends)])]
    scatter x10 -> x0, local copies, waits for them, and re-layouts: 18.9 us -> none
    all_to_all x1 -> x0, starting transfers between devices: 18.1 us -> none  [body(): lax.all_to_all(sinogram, ('ang', 'sx'), split_axis=2, concat_axis=0, tile...]
    ppermute x8 -> x0, waiting for transfers between devices: 17.1 us -> none  [the longest x4 12.8 us: with_halo(): lax.ppermute(head, axis, [((i + 1) % count, i) for i in range(ends)])]
    dot_general x4 -> x0, matrix products: 16 us -> none  [the longest x2 8.42 us: right_product(): jnp.einsum('btrc,tcsq->bsrq', fields, matrix, preferred_element_type=jnp....]
    scatter x5 -> x0, other arithmetic: 14.5 us -> none
  transfers between devices with their start and end apart: 10 -> 0, of which waited for: 6 -> 0; matrix products, arithmetic and copies ran while one was open for 7% -> 0% of each run, Pallas kernels for 0% -> 0%
where the time goes in v1:
time: 78.7 us; the launch traced here: 78.2 us
  Pallas kernels  64.8 us (82%)
  local copies, waits for them, and re-layouts  12.7 us (16%)
    pallas_call x1, Pallas kernels, body(): pl.pallas_call(functools.partial(regroup_kernel, angles), out_shape=(shap...  41 us
    pallas_call x1, Pallas kernels, body(): pl.pallas_call(strips_kernel, out_shape=rim_shapes, in_specs=[hbm], out_s...  13.3 us
    unnamed x24, local copies, waits for them, and re-layouts  12.7 us
    pallas_call x1, Pallas kernels, body(): pl.pallas_call(functools.partial(patch_kernel, angles), out_shape=(shape(...  7.85 us
    pallas_call x1, Pallas kernels, body(): pl.pallas_call(functools.partial(finish_kernel, angles), out_shape=(shape...  2.69 us

profile of v1, /device:TPU:1, one launch (start us, length us, event | category | flops | bytes accessed | tf_op | source)
XLA Modules:
  0.0 78.2 jit_solution(18117873024329131946)
XLA Ops:
  0.6 13.3 %shard_map.112 = (bf16[2,64,512]{2,1,0:T(8,128)(2,1)}, bf16[2,512,128]{2,1,0:T(8,128)(2,1)}, bf16[2,64,128]{2,1,0:T(8,128)(2,1)}) custom-call(bf16[1,2,512,512]{3,2,1,0:T(8,128)(2,1)} %obj_ref.3), custom_call_target="tpu_custom_call" | custom-call | tf_op jit(solution)/shard_map/pallas_call | solution.py:462
  13.9 0.0 copy-start
  13.9 2.2 %copy-done = bf16[8,16,128,128]{3,2,1,0:T(8,128)(2,1)S(1)} copy-done((bf16[8,16,128,128]{3,2,1,0:T(8,128)(2,1)S(1)}, bf16[8,16,128,128]{3,2,1,0:T(8,128)(2,1)}, u32[]{:S(2)}) %copy-start) | copy-done | bytes 4194328
  16.1 0.0 copy-start.1
  16.1 1.2 %copy-done.1 = bf16[1,2,512,512]{3,2,1,0:T(8,128)(2,1)S(1)} copy-done((bf16[1,2,512,512]{3,2,1,0:T(8,128)(2,1)S(1)}, bf16[1,2,512,512]{3,2,1,0:T(8,128)(2,1)}, u32[]{:S(2)}) %copy-start.1) | copy-done | bytes 1048600
  17.3 0.0 copy-start.2
  17.3 1.2 %copy-done.2 = f32[2,2,256,256]{3,2,1,0:T(8,128)S(1)} copy-done((f32[2,2,256,256]{3,2,1,0:T(8,128)S(1)}, f32[2,2,256,256]{3,2,1,0:T(8,128)}, u32[]{:S(2)}) %copy-start.2) | copy-done | bytes 1048600
  18.6 0.0 copy-start.3
  18.6 1.0 %copy-done.3 = bf16[512,512]{1,0:T(8,128)(2,1)S(1)} copy-done((bf16[512,512]{1,0:T(8,128)(2,1)S(1)}, bf16[512,512]{1,0:T(8,128)(2,1)}, u32[]{:S(2)}) %copy-start.3) | copy-done | bytes 524312
  19.6 0.0 copy-start.4
  19.6 1.0 %copy-done.4 = bf16[512,512]{1,0:T(8,128)(2,1)S(1)} copy-done((bf16[512,512]{1,0:T(8,128)(2,1)S(1)}, bf16[512,512]{1,0:T(8,128)(2,1)}, u32[]{:S(2)}) %copy-start.4) | copy-done | bytes 524312
  20.6 0.0 copy-start.5
  20.6 1.0 %copy-done.5 = bf16[1920,128]{1,0:T(8,128)(2,1)S(1)} copy-done((bf16[1920,128]{1,0:T(8,128)(2,1)S(1)}, bf16[1920,128]{1,0:T(8,128)(2,1)}, u32[]{:S(2)}) %copy-start.5) | copy-done | bytes 491544
  21.7 0.0 copy-start.6
  21.7 0.9 %copy-done.6 = bf16[1,1,1,2,256,256]{5,4,3,2,1,0:T(8,128)(2,1)S(1)} copy-done((bf16[1,1,1,2,256,256]{5,4,3,2,1,0:T(8,128)(2,1)S(1)}, bf16[1,1,1,2,256,256]{5,4,3,2,1,0:T(8,128)(2,1)}, u32[]{:S(2)}) %copy-start.6) | copy-done | bytes 262168
  22.6 0.0 copy-start.7
  22.6 0.9 %copy-done.7 = bf16[2,512,128]{2,1,0:T(8,128)(2,1)S(1)} copy-done((bf16[2,512,128]{2,1,0:T(8,128)(2,1)S(1)}, bf16[2,512,128]{2,1,0:T(8,128)(2,1)}, u32[]{:S(2)}) %copy-start.7) | copy-done | bytes 262168
  23.6 0.0 copy-start.8
  23.6 0.9 %copy-done.8 = bf16[2,64,512]{2,1,0:T(8,128)(2,1)S(1)} copy-done((bf16[2,64,512]{2,1,0:T(8,128)(2,1)S(1)}, bf16[2,64,512]{2,1,0:T(8,128)(2,1)}, u32[]{:S(2)}) %copy-start.8) | copy-done | bytes 131096
  24.5 0.0 copy-start.9
  24.5 0.8 copy-done.9
  25.2 0.0 copy-start.10
  25.2 0.7 copy-done.10
  25.9 0.0 copy-start.11
  25.9 0.7 copy-done.11
  26.6 7.8 %shard_map.113 = (f32[2,512,512]{2,1,0:T(8,128)S(1)}, bf16[2,64,512]{2,1,0:T(8,128)(2,1)S(1)}, bf16[2,512,128]{2,1,0:T(8,128)(2,1)S(1)}, bf16[2,64,128]{2,1,0:T(...) custom-call(s32[1,1,1,2,2]{4,3,2,1,0:T(2,128)S(1)} %copy-done.11, ...), custom_call_target="tpu_custom_call" | custom-call | tf_op jit(solution)/shard_map/pallas_call | solution.py:470
  34.5 41.0 %shard_map.114 = (f32[2,512,512]{2,1,0:T(8,128)S(1)}, bf16[4,256,256]{2,1,0:T(8,128)(2,1)S(1)}, bf16[128,8,256]{2,1,0:T(8,128)(2,1)S(1)}) custom-call(f32[2,512,512]{2,1,0:T(8,128)S(1)} %get-tuple-element.19.og_ref, bf16[2,64,512]{2,1,0:T(8,128)(2,1)S(1)} %get-tuple-element.20.row_ref, bf16[2,512,128]{2,1,0:T(8,128)(2,1)S(1)} %get-tuple-element.21.col_ref, ...), custom_call_target="tpu_custom_call" | custom-call | tf_op jit(solution)/shard_map/pallas_call | solution.py:501
  75.5 2.7 %shard_map.115 = (f32[1,2,512,512]{3,2,1,0:T(8,128)}, f32[1,2,2,256,256]{4,3,2,1,0:T(8,128)}, f32[1,4,2,1024]{3,2,1,0:T(2,128)}) custom-call(s32[8,16]{1,0:T(8,128)S(1)} %copy-done.10, f32[2,512,512]{2,1,0:T(8,128)S(1)} %get-tuple-element.26.og_ref, bf16[4,256,256]{2,1,0:T(8,128)(2,1)S(1)} %get-tuple-element.27.total_ref, ...), custom_call_target="tpu_custom_call" | custom-call | tf_op jit(solution)/shard_map/pallas_call | solution.py:529
Async XLA Ops:
  13.9 2.2 %copy-start = (bf16[8,16,128,128]{3,2,1,0:T(8,128)(2,1)S(1)}, bf16[8,16,128,128]{3,2,1,0:T(8,128)(2,1)}, u32[]{:S(2)}) copy-start(bf16[8,16,128,128]{3,2,1,0:T(8,128)(2,1)} %bv_ref.1) | copy-start | bytes 12582916
  16.1 1.2 %copy-start.1 = (bf16[1,2,512,512]{3,2,1,0:T(8,128)(2,1)S(1)}, bf16[1,2,512,512]{3,2,1,0:T(8,128)(2,1)}, u32[]{:S(2)}) copy-start(bf16[1,2,512,512]{3,2,1,0:T(8,128)(2,1)} %obj_ref.3) | copy-start | bytes 3145732
  17.3 1.2 %copy-start.2 = (f32[2,2,256,256]{3,2,1,0:T(8,128)S(1)}, f32[2,2,256,256]{3,2,1,0:T(8,128)}, u32[]{:S(2)}) copy-start(f32[2,2,256,256]{3,2,1,0:T(8,128)} %probe_ref.1) | copy-start | bytes 3145732
  18.6 1.0 %copy-start.3 = (bf16[512,512]{1,0:T(8,128)(2,1)S(1)}, bf16[512,512]{1,0:T(8,128)(2,1)}, u32[]{:S(2)}) copy-start(bf16[512,512]{1,0:T(8,128)(2,1)} %constant.7.clone.bwd_ref) | copy-start | bytes 1572868
  19.6 1.0 %copy-start.4 = (bf16[512,512]{1,0:T(8,128)(2,1)S(1)}, bf16[512,512]{1,0:T(8,128)(2,1)}, u32[]{:S(2)}) copy-start(bf16[512,512]{1,0:T(8,128)(2,1)} %constant.6.clone.fwd_ref) | copy-start | bytes 1572868
  20.6 1.0 %copy-start.5 = (bf16[1920,128]{1,0:T(8,128)(2,1)S(1)}, bf16[1920,128]{1,0:T(8,128)(2,1)}, u32[]{:S(2)}) copy-start(bf16[1920,128]{1,0:T(8,128)(2,1)} %constant.8.clone.ramp_ref) | copy-start | bytes 1474564
  21.7 0.9 %copy-start.6 = (bf16[1,1,1,2,256,256]{5,4,3,2,1,0:T(8,128)(2,1)S(1)}, bf16[1,1,1,2,256,256]{5,4,3,2,1,0:T(8,128)(2,1)}, u32[]{:S(2)}) copy-start(bf16[1,1,1,2,256,256]{5,4,3,2,1,0:T(8,128)(2,1)} %data_ref.1) | copy-start | bytes 786436
  22.6 0.9 %copy-start.7 = (bf16[2,512,128]{2,1,0:T(8,128)(2,1)S(1)}, bf16[2,512,128]{2,1,0:T(8,128)(2,1)}, u32[]{:S(2)}) copy-start(bf16[2,512,128]{2,1,0:T(8,128)(2,1)} %get-tuple-element.17.halo_col) | copy-start | bytes 786436
  23.6 0.9 %copy-start.8 = (bf16[2,64,512]{2,1,0:T(8,128)(2,1)S(1)}, bf16[2,64,512]{2,1,0:T(8,128)(2,1)}, u32[]{:S(2)}) copy-start(bf16[2,64,512]{2,1,0:T(8,128)(2,1)} %get-tuple-element.16.halo_row) | copy-start | bytes 393220
  24.5 0.8 copy-start.9
  25.2 0.7 copy-start.10
  25.9 0.7 copy-start.11

commit v2 on v1

--- a/solution.py
+++ b/solution.py
@@ -41,17 +41,29 @@
     return values.astype(BF)
 
 
-def strips_kernel(obj_ref, row_out, col_out, cor_out, send_sem, recv_sem):
+def swap_halves(cells):
+    return pltpu.roll(cells, BLK // 2, cells.ndim - 1)
+
+
+def strips_kernel(obj_ref, row_out, col_out, cor_out, block, packed, load_sem, send_sem, recv_sem):
     ang, sy, sx = lax.axis_index("ang"), lax.axis_index("sy"), lax.axis_index("sx")
     oy, ox = 1 - sy, 1 - sx
     devices = [(ang, oy, sx), (ang, sy, ox), (ang, oy, ox)]
+    rows = pl.ds(pl.multiple_of((TILE - RIM) * oy, RIM), RIM)
+    cols = pl.ds(pl.multiple_of((TILE - BLK) * ox, BLK), BLK)
+    load = pltpu.make_async_copy(obj_ref.at[0, :, :, cols], block, load_sem)
+    load.start()
     barrier = pltpu.get_barrier_semaphore()
     for dev in devices:
         pl.semaphore_signal(barrier, inc=1, device_id=dev, device_id_type=MESH)
+    load.wait()
+    real, imag = block[0].astype(F32), block[1].astype(F32)
+    low = lax.broadcasted_iota(jnp.int32, (TILE, BLK), 1) < RIM
+    packed[...] = jnp.where(
+        low, jnp.where(sx == 0, swap_halves(real), real), jnp.where(sx == 0, imag, swap_halves(imag))
+    ).astype(BF)
     pl.semaphore_wait(barrier, 3)
-    rows = pl.ds(pl.multiple_of((TILE - RIM) * oy, RIM), RIM)
-    cols = pl.ds(pl.multiple_of((TILE - BLK) * ox, BLK), BLK)
-    sources = [obj_ref.at[0, :, rows, :], obj_ref.at[0, :, :, cols], obj_ref.at[0, :, rows, cols]]
+    sources = [obj_ref.at[0, :, rows, :], packed, packed.at[rows]]
     copies = [
         pltpu.make_async_remote_copy(
             src_ref=src, dst_ref=dst, send_sem=send_sem.at[i], recv_sem=recv_sem.at[i],
@@ -70,7 +82,7 @@
     pos_ref, bi_ref,
     obj_ref, halo_row, halo_col, halo_cor, probe_ref, data_ref, fwd_ref, bwd_ref, ramp_ref, bv_ref,
     og_out, row_out, col_out, cor_out, part_out, ramp_out, bv_out,
-    big, probe, data, fwd, bwd, ramp, bv,
+    big, side, probe, data, fwd, bwd, ramp, bv,
     win, patch, exits, half, far, chi, placed, og,
     rim_row, rim_col, rim_cor, part,
     load_sem, pick_sem, out_sem,
@@ -85,8 +97,8 @@
             [
                 (obj_ref.at[0], big.at[:, pl.ds(RIM, TILE), pl.ds(BLK, TILE)]),
                 (halo_row, big.at[:, dst_row, pl.ds(BLK, TILE)]),
-                (halo_col, big.at[:, pl.ds(RIM, TILE), dst_col]),
-                (halo_cor, big.at[:, dst_row, dst_col]),
+                (halo_col, side.at[pl.ds(RIM, TILE)]),
+                (halo_cor, side.at[dst_row]),
                 (probe_ref, probe),
                 (fwd_ref, fwd),
                 (bwd_ref, bwd),
@@ -126,8 +138,13 @@
         )
     for copy in picks:
         copy.start()
+    side[pl.ds(pl.multiple_of((ROWS - RIM) * sy, RIM), RIM), :] = jnp.zeros((RIM, BLK), BF)
     for copy in loads:
         copy.wait()
+    wide = side[...].astype(F32)
+    turned = swap_halves(wide)
+    big[0, :, dst_col] = jnp.where(sx == 1, turned, wide).astype(BF)
+    big[1, :, dst_col] = jnp.where(sx == 1, wide, turned).astype(BF)
 
     def corner(p):
         return pos_ref[0, 0, 0, p, 0], pos_ref[0, 0, 0, p, 1] + RIM
@@ -213,13 +230,16 @@
     for c in range(2):
         for b in range(4):
             rim_row[c, :, b * BLK : (b + 1) * BLK] = cells_at(c, rim_chunk, b + 1).astype(BF)
-        rim_cor[c] = cells_at(c, rim_chunk, rim_block).astype(BF)
+
+    def packed_rim(row_chunk):
+        real, imag = (cells_at(c, row_chunk, rim_block) for c in range(2))
+        kept, moved = jnp.where(sx == 0, real, imag), jnp.where(sx == 0, imag, real)
+        return (kept + swap_halves(moved)).astype(BF)
+
+    rim_cor[...] = packed_rim(rim_chunk)
 
     def rim_columns(r, carry):
-        for c in range(2):
-            rim_col[c, pl.ds(pl.multiple_of(r * RIM, RIM), RIM), :] = cells_at(
-                c, r + 1, rim_block
-            ).astype(BF)
+        rim_col[pl.ds(pl.multiple_of(r * RIM, RIM), RIM), :] = packed_rim(r + 1)
         return carry
 
     lax.fori_loop(0, 8, rim_columns, 0)
@@ -269,9 +289,9 @@
     angles,
     og_ref, row_ref, col_ref, cor_ref, part_ref, ramp_ref, bv_ref,
     og_out, total_out, inbox_out,
-    og, part, ramp, bv, got_row, got_col, got_cor, part_got, total_send, total, sino, msgs, inbox,
-    load_sem, rim_send, rim_recv,
-    part_ssem, part_rsem, tot_ssem, tot_rsem, a2a_send, a2a_recv, own_sem, out_sem,
+    og, part, ramp, bv, got_row, got_col, got_cor, half_got, half_sum, quarter_send, quarter_got, total,
+    sino, msgs, inbox,
+    load_sem, rim_send, rim_recv, part_ssem, part_rsem, word_sem, a2a_send, a2a_recv, own_sem, out_sem,
 ):
     ang, sy, sx = lax.axis_index("ang"), lax.axis_index("sy"), lax.axis_index("sx")
     oy, ox = 1 - sy, 1 - sx
@@ -280,26 +300,22 @@
     tile = sy * 2 + sx
 
     barrier = pltpu.get_barrier_semaphore()
-    for dev in ((ang, oy, sx), (ang, oy, ox)):
+    steps = group.bit_length() - 1
+    partners = []
+    for r in range(steps):
+        d = jnp.bitwise_xor(me, 1 << r)
+        partners.append((d >> 1, sy, d & 1))
+    for dev in [(ang, oy, sx), (ang, oy, ox)] + partners:
         pl.semaphore_signal(barrier, inc=1, device_id=dev, device_id_type=MESH)
-
-    def greet(k, carry):
-        d = lax.rem(me + k, group)
-        pl.semaphore_signal(
-            barrier, inc=1, device_id=(d // 2, sy, lax.rem(d, 2)), device_id_type=MESH
-        )
-        return carry
-
-    lax.fori_loop(1, group, greet, 0)
     loads = [
         pltpu.make_async_copy(src, dst, load_sem.at[i])
         for i, (src, dst) in enumerate(
-            [(og_ref, og), (ramp_ref, ramp), (bv_ref, bv), (part_ref.at[tile], part)]
+            [(og_ref, og), (ramp_ref, ramp), (bv_ref, bv), (part_ref.at[pl.ds(2 * sy, 2)], part)]
         )
     ]
     for copy in loads:
         copy.start()
-    pl.semaphore_wait(barrier, group + 1)
+    pl.semaphore_wait(barrier, steps + 2)
 
     rims = [
         pltpu.make_async_remote_copy(
@@ -316,27 +332,42 @@
     ]
     for copy in rims:
         copy.start()
-    others = [(sy, ox), (oy, sx), (oy, ox)]
-    part_copies = [
-        pltpu.make_async_remote_copy(
-            src_ref=part_ref.at[ty * 2 + tx], dst_ref=part_got.at[i],
-            send_sem=part_ssem.at[i], recv_sem=part_rsem.at[i],
-            device_id=(ang, ty, tx), device_id_type=MESH,
-        )
-        for i, (ty, tx) in enumerate(others)
-    ]
-    for copy in part_copies:
-        copy.start()
+    def exchange(i, src, dst, dev):
+        return pltpu.make_async_remote_copy(
+            src_ref=src, dst_ref=dst, send_sem=part_ssem.at[i], recv_sem=part_rsem.at[i],
+            device_id=dev, device_id_type=MESH,
+        )
+
+    across, beside = (ang, oy, ox), (ang, sy, ox)
+    halves = exchange(0, part_ref.at[pl.ds(2 * oy, 2)], half_got, across)
+    halves.start()
     for copy in loads:
         copy.wait()
+    for r in range(steps):
+        pl.semaphore_signal(word_sem.at[r], inc=1, device_id=partners[r], device_id_type=MESH)
+        pl.semaphore_wait(word_sem.at[r], 1)
     for copy in rims:
         copy.wait()
+    halves.wait()
+    half_sum[...] = part[...].astype(F32) + half_got[...].astype(F32)
+    quarter_send[...] = half_sum[ox].astype(BF)
+    quarters = exchange(1, quarter_send, quarter_got, beside)
+    quarters.start()
     row_at = pl.ds(pl.multiple_of((TILE - RIM) * oy, RIM), RIM)
     col_at = pl.ds(pl.multiple_of((TILE - BLK) * ox, BLK), BLK)
     for c in range(2):
         og[c, row_at, :] = og[c, row_at, :] + got_row[c].astype(F32)
-        og[c, :, col_at] = og[c, :, col_at] + got_col[c].astype(F32)
-        og[c, row_at, col_at] = og[c, row_at, col_at] + got_cor[c].astype(F32)
+    first = lax.broadcasted_iota(jnp.int32, (TILE, BLK), 1) < RIM
+    for got, at in ((got_col, pl.ds(0, TILE)), (got_cor, row_at)):
+        wide = got[...].astype(F32)
+        turned = swap_halves(wide)
+        low = first[: wide.shape[0]]
+        added = (
+            jnp.where(sx == 1, jnp.where(low, wide, 0.0), jnp.where(low, 0.0, turned)),
+            jnp.where(sx == 1, jnp.where(low, turned, 0.0), jnp.where(low, 0.0, wide)),
+        )
+        for c in range(2):
+            og[c, at, col_at] = og[c, at, col_at] + added[c]
     og_copy = pltpu.make_async_copy(og, og_out, out_sem.at[0])
     og_copy.start()
 
@@ -366,30 +397,21 @@
     own = pltpu.make_async_copy(msgs.at[ang, sx], inbox.at[me], own_sem)
     own.start()
 
-    for copy in part_copies:
-        copy.wait()
-    summed = part[...].astype(F32) + part_got[0].astype(F32) + part_got[1].astype(F32) + part_got[2].astype(F32)
-    total_send[...] = summed.astype(BF)
-    total[tile] = total_send[...]
-    total_copies = [
-        pltpu.make_async_remote_copy(
-            src_ref=total_send, dst_ref=total.at[tile],
-            send_sem=tot_ssem.at[i], recv_sem=tot_rsem.at[i],
-            device_id=(ang, ty, tx), device_id_type=MESH,
-        )
-        for i, (ty, tx) in enumerate(others)
-    ]
-    for copy in total_copies:
-        copy.start()
-
+    quarters.wait()
+    total[tile] = (half_sum[sx] + quarter_got[...].astype(F32)).astype(BF)
+    shared = exchange(2, total.at[tile], total.at[tile], beside)
+    shared.start()
+    shared.wait()
+    mine = pl.ds(2 * sy, 2)
+    rest = exchange(3, total.at[mine], total.at[mine], across)
+    rest.start()
     own.wait()
     pltpu.make_async_copy(
         inbox.at[pl.ds(0, group - 1)], inbox.at[pl.ds(0, group - 1)], a2a_recv
     ).wait()
     inbox_copy = pltpu.make_async_copy(inbox, inbox_out, out_sem.at[1])
     inbox_copy.start()
-    for copy in total_copies:
-        copy.wait()
+    rest.wait()
     total_copy = pltpu.make_async_copy(total, total_out, out_sem.at[2])
     total_copy.start()
     pltpu.make_async_copy(
@@ -453,19 +475,23 @@
     group = 2 * angles
     dma = pltpu.SemaphoreType.DMA
     smem = pl.BlockSpec(memory_space=pltpu.SMEM)
-    hbm = pl.BlockSpec(memory_space=pl.ANY)
+    hbm = pl.BlockSpec(memory_space=pltpu.HBM)
 
     def shape(dims, kind):
         return jax.ShapeDtypeStruct(dims, kind)
 
-    rim_shapes = (shape((2, RIM, TILE), BF), shape((2, TILE, BLK), BF), shape((2, RIM, BLK), BF))
+    rim_shapes = (shape((2, RIM, TILE), BF), shape((TILE, BLK), BF), shape((RIM, BLK), BF))
     halos = pl.pallas_call(
         strips_kernel,
         out_shape=rim_shapes,
         in_specs=[hbm],
         out_specs=[hbm] * 3,
-        scratch_shapes=[dma((3,)), dma((3,))],
-        compiler_params=pltpu.CompilerParams(collective_id=0, has_side_effects=True),
+        scratch_shapes=[
+            pltpu.VMEM((2, TILE, BLK), BF), pltpu.VMEM((TILE, BLK), BF), dma, dma((3,)), dma((3,)),
+        ],
+        compiler_params=pltpu.CompilerParams(
+            collective_id=0, has_side_effects=True, vmem_limit_bytes=62 * 1024 * 1024
+        ),
     )(objects)
     og_part, row, col, cor, parts, ramp_two, bv_two = pl.pallas_call(
         functools.partial(patch_kernel, angles),
@@ -476,6 +502,7 @@
         out_specs=[hbm] * 7,
         scratch_shapes=[
             pltpu.VMEM((2, ROWS, COLS), BF),
+            pltpu.VMEM((ROWS, BLK), BF),
             pltpu.VMEM((2, 2, PATCH, PATCH), F32),
             pltpu.VMEM((2, PATCH, PATCH), BF),
             pltpu.VMEM((512, 512), BF),
@@ -491,12 +518,12 @@
             pltpu.VMEM((4, 5, 384, BLK), F32),
             pltpu.VMEM((2, TILE, TILE), F32),
             pltpu.VMEM((2, RIM, TILE), BF),
-            pltpu.VMEM((2, TILE, BLK), BF),
-            pltpu.VMEM((2, RIM, BLK), BF),
+            pltpu.VMEM((TILE, BLK), BF),
+            pltpu.VMEM((RIM, BLK), BF),
             pltpu.VMEM((4, PATCH, PATCH), BF),
             dma((8,)), dma((4,)), dma((7,)),
         ],
-        compiler_params=pltpu.CompilerParams(vmem_limit_bytes=40 * 1024 * 1024),
+        compiler_params=pltpu.CompilerParams(vmem_limit_bytes=62 * 1024 * 1024),
     )(positions, block_index, objects, *halos, probe, data, forward, backward, ramp, block_values)
     og, total, inbox = pl.pallas_call(
         functools.partial(regroup_kernel, angles),
@@ -507,23 +534,25 @@
         out_specs=[hbm] * 3,
         scratch_shapes=[
             pltpu.VMEM((2, TILE, TILE), F32),
-            pltpu.VMEM((PATCH, PATCH), BF),
+            pltpu.VMEM((2, PATCH, PATCH), BF),
             pltpu.VMEM((2, TILE, BLK), BF),
             pltpu.VMEM((2, BLK, BLK), BF),
             pltpu.VMEM((2, RIM, TILE), BF),
-            pltpu.VMEM((2, TILE, BLK), BF),
-            pltpu.VMEM((2, RIM, BLK), BF),
-            pltpu.VMEM((3, PATCH, PATCH), BF),
+            pltpu.VMEM((TILE, BLK), BF),
+            pltpu.VMEM((RIM, BLK), BF),
+            pltpu.VMEM((2, PATCH, PATCH), BF),
+            pltpu.VMEM((2, PATCH, PATCH), F32),
+            pltpu.VMEM((PATCH, PATCH), BF),
             pltpu.VMEM((PATCH, PATCH), BF),
             pltpu.VMEM((4, PATCH, PATCH), BF),
             pltpu.VMEM((2 * TILE, TILE), BF),
             pltpu.VMEM((group // 2, 2, 8, 2 * BLK), BF),
             pltpu.VMEM((group, 8, 2 * BLK), BF),
-            dma((4,)), dma((3,)), dma((3,)),
-            dma((3,)), dma((3,)), dma((3,)), dma((3,)), dma, dma, dma, dma((3,)),
+            dma((4,)), dma((3,)), dma((3,)), dma((4,)), dma((4,)),
+            pltpu.SemaphoreType.REGULAR((group.bit_length() - 1,)), dma, dma, dma, dma((3,)),
         ],
         compiler_params=pltpu.CompilerParams(
-            collective_id=1, has_side_effects=True, vmem_limit_bytes=40 * 1024 * 1024
+            collective_id=1, has_side_effects=True, vmem_limit_bytes=62 * 1024 * 1024
         ),
     )(og_part, row, col, cor, parts, ramp_two, bv_two)
     return pl.pallas_call(
@@ -542,7 +571,7 @@
             pltpu.SMEM((angles,), jnp.int32),
             dma((2,)), dma((8,)), dma((2,)),
         ],
-        compiler_params=pltpu.CompilerParams(vmem_limit_bytes=40 * 1024 * 1024),
+        compiler_params=pltpu.CompilerParams(vmem_limit_bytes=62 * 1024 * 1024),
     )(block_index, og, total, inbox)
 
 

time: 78.7 us -> 62.8 us (0.80)
  local copies, waits for them, and re-layouts: 12.7 us -> 0 us
  Pallas kernels: 64.8 us -> 61.7 us
    unnamed x24 -> x0, local copies, waits for them, and re-layouts: 12.7 us -> none
    pallas_call x1, Pallas kernels: 41 us -> 36.7 us  [body(): pl.pallas_call(functools.partial(regroup_kernel, angles), out_shape=(shap...]
    pallas_call x1, Pallas kernels: 13.3 us -> 10.4 us  [body(): pl.pallas_call(strips_kernel, out_shape=rim_shapes, in_specs=[hbm], out_s...]
    pallas_call x1, Pallas kernels: 7.85 us -> 10.3 us  [body(): pl.pallas_call(functools.partial(patch_kernel, angles), out_shape=(shape(...]
    pallas_call x1, Pallas kernels: 2.69 us -> 4.24 us  [body(): pl.pallas_call(functools.partial(finish_kernel, angles), out_shape=(shape...]
where the time goes in v2:
time: 62.8 us; the launch traced here: 62.3 us
  Pallas kernels  61.7 us (98%)
  between operations  0.65 us (1%)
    pallas_call x1, Pallas kernels, body(): pl.pallas_call(functools.partial(regroup_kernel, angles), out_shape=(shap...  36.7 us
    pallas_call x1, Pallas kernels, body(): pl.pallas_call(strips_kernel, out_shape=rim_shapes, in_specs=[hbm], out_s...  10.4 us
    pallas_call x1, Pallas kernels, body(): pl.pallas_call(functools.partial(patch_kernel, angles), out_shape=(shape(...  10.3 us
    pallas_call x1, Pallas kernels, body(): pl.pallas_call(functools.partial(finish_kernel, angles), out_shape=(shape...  4.24 us

profile of v2, /device:TPU:1, one launch (start us, length us, event | category | flops | bytes accessed | tf_op | source)
XLA Modules:
  0.0 62.3 jit_solution(13810667542611588516)
XLA Ops:
  0.6 10.4 %shard_map.112 = (bf16[2,64,512]{2,1,0:T(8,128)(2,1)}, bf16[512,128]{1,0:T(8,128)(2,1)}, bf16[64,128]{1,0:T(8,128)(2,1)}) custom-call(bf16[1,2,512,512]{3,2,1,0:T(8,128)(2,1)} %obj_ref.3), custom_call_target="tpu_custom_call" | custom-call | tf_op jit(solution)/shard_map/pallas_call | solution.py:484
  11.0 10.3 %shard_map.113 = (f32[2,512,512]{2,1,0:T(8,128)}, bf16[2,64,512]{2,1,0:T(8,128)(2,1)}, bf16[512,128]{1,0:T(8,128)(2,1)}, bf16[64,128]{1,0:T(8,128)(2,1)}, bf16[4...) custom-call(s32[1,1,1,2,2]{4,3,2,1,0:T(2,128)} %pos_ref.1, s32[8,16]{1,0:T(8,128)} %bi_ref.3, ...), custom_call_target="tpu_custom_call" | custom-call | tf_op jit(solution)/shard_map/pallas_call | solution.py:496
  21.3 36.7 %shard_map.114 = (f32[2,512,512]{2,1,0:T(8,128)}, bf16[4,256,256]{2,1,0:T(8,128)(2,1)}, bf16[128,8,256]{2,1,0:T(8,128)(2,1)}) custom-call(f32[2,512,512]{2,1,0:T(8,128)} %get-tuple-element.19.og_ref, bf16[2,64,512]{2,1,0:T(8,128)(2,1)} %get-tuple-element.20.row_ref, bf16[512,128]{1,0:T(8,128)(2,1)} %get-tuple-element.21.col_ref, ...), custom_call_target="tpu_custom_call" | custom-call | tf_op jit(solution)/shard_map/pallas_call | solution.py:528
  58.1 4.2 %shard_map.115 = (f32[1,2,512,512]{3,2,1,0:T(8,128)}, f32[1,2,2,256,256]{4,3,2,1,0:T(8,128)}, f32[1,4,2,1024]{3,2,1,0:T(2,128)}) custom-call(s32[8,16]{1,0:T(8,128)} %bi_ref.3, f32[2,512,512]{2,1,0:T(8,128)} %get-tuple-element.26.og_ref, bf16[4,256,256]{2,1,0:T(8,128)(2,1)} %get-tuple-element.27.total_ref, bf16[128,8,256]{2,1,0:T(8,128)(2,1)} %get-tuple-element.28.inbox_ref), custom_call_target="tpu_custom_call" | custom-call | tf_op jit(solution)/shard_map/pallas_call | solution.py:558

commit v3 on v2

--- a/solution.py
+++ b/solution.py
@@ -14,7 +14,9 @@
 BLK = 128
 TILE = 512
 ROWS = 640
+SPAN = 640
 COLS = 768
+SECOND = (0, 2, 3, 1)
 MESH = pl.DeviceIdType.MESH
 BF = jnp.bfloat16
 F32 = jnp.float32
@@ -81,10 +83,10 @@
     angles,
     pos_ref, bi_ref,
     obj_ref, halo_row, halo_col, halo_cor, probe_ref, data_ref, fwd_ref, bwd_ref, ramp_ref, bv_ref,
-    og_out, row_out, col_out, cor_out, part_out, ramp_out, bv_out,
+    og_out, row_out, col_out, cor_out, part_out, ramp_out, bv_out, sino_out,
     big, side, probe, data, fwd, bwd, ramp, bv,
     win, patch, exits, half, far, chi, placed, og,
-    rim_row, rim_col, rim_cor, part,
+    rim_row, rim_col, rim_cor, part, sino,
     load_sem, pick_sem, out_sem,
 ):
     ang, sy, sx = lax.axis_index("ang"), lax.axis_index("sy"), lax.axis_index("sx")
@@ -129,9 +131,9 @@
     named[0] = (jnp.maximum(named[0][0], 0), named[0][1])
     picks = []
     for s, (entry, column) in enumerate(named):
-        at = pl.multiple_of((7 - column + 4 * sx) * BLK, BLK)
+        at = pl.multiple_of((7 - column + 3 * sx) * BLK, BLK)
         picks.append(
-            pltpu.make_async_copy(ramp_ref.at[pl.ds(at, TILE), :], ramp.at[s], pick_sem.at[2 * s])
+            pltpu.make_async_copy(ramp_ref.at[pl.ds(at, SPAN), :], ramp.at[s], pick_sem.at[2 * s])
         )
         picks.append(
             pltpu.make_async_copy(bv_ref.at[entry >> 4, entry & 15], bv.at[s], pick_sem.at[2 * s + 1])
@@ -248,7 +250,7 @@
         for i, (src, dst) in enumerate(
             [
                 (rim_row, row_out), (rim_col, col_out), (rim_cor, cor_out),
-                (og, og_out), (part, part_out), (ramp, ramp_out), (bv, bv_out),
+                (og, og_out), (part, part_out), (ramp, ramp_out), (bv, bv_out), (sino, sino_out),
             ]
         )
     ]
@@ -256,30 +258,39 @@
         copy.start()
     for copy in picks:
         copy.wait()
-    for copy in outs[5:]:
-        copy.start()
+    for copy in outs[5:7]:
+        copy.start()
+
+    for c in range(2):
+        for b in range(5):
+            sino[2 * TILE + c * RIM : 2 * TILE + (c + 1) * RIM, b * BLK : (b + 1) * BLK] = cells_at(
+                c, rim_chunk, b + ox
+            ).astype(BF)
 
     def interior(r, carry):
+        rows = pl.ds(pl.multiple_of(r * RIM, RIM), RIM)
         for c in range(2):
             for b in range(4):
-                og[c, pl.ds(pl.multiple_of(r * RIM, RIM), RIM), b * BLK : (b + 1) * BLK] = cells_at(
-                    c, r + 1, b + 1
-                )
+                og[c, rows, b * BLK : (b + 1) * BLK] = cells_at(c, r + 1, b + 1)
+            for b in range(5):
+                sino[pl.ds(pl.multiple_of(c * TILE + r * RIM, RIM), RIM), b * BLK : (b + 1) * BLK] = cells_at(
+                    c, r + 1, b + ox
+                ).astype(BF)
         return carry
 
     lax.fori_loop(0, 8, interior, 0)
-
+    outs[7].start()
     outs[3].start()
 
     for m in range(2):
-        part[2 * m] = (
-            patch[0, 0] * chi[0, m, :, 0:PATCH] + patch[0, 1] * chi[0, m, :, PATCH:]
-            + patch[1, 0] * chi[1, m, :, 0:PATCH] + patch[1, 1] * chi[1, m, :, PATCH:]
-        ).astype(BF)
-        part[2 * m + 1] = (
-            patch[0, 0] * chi[0, m, :, PATCH:] - patch[0, 1] * chi[0, m, :, 0:PATCH]
-            + patch[1, 0] * chi[1, m, :, PATCH:] - patch[1, 1] * chi[1, m, :, 0:PATCH]
-        ).astype(BF)
+        real, imag = (
+            patch[0, 0] * chi[0, m, :, a] + sign * patch[0, 1] * chi[0, m, :, b]
+            + patch[1, 0] * chi[1, m, :, a] + sign * patch[1, 1] * chi[1, m, :, b]
+            for a, b, sign in ((slice(0, PATCH), slice(PATCH, 512), 1.0), (slice(PATCH, 512), slice(0, PATCH), -1.0))
+        )
+        for q, terms in ((2 * m, real), (2 * m + 1, imag)):
+            part[0, q] = terms[0:BLK].astype(BF)
+            part[1, SECOND[q]] = terms[BLK:].astype(BF)
     outs[4].start()
     for copy in outs:
         copy.wait()
@@ -287,36 +298,132 @@
 
 def regroup_kernel(
     angles,
-    og_ref, row_ref, col_ref, cor_ref, part_ref, ramp_ref, bv_ref,
-    og_out, total_out, inbox_out,
-    og, part, ramp, bv, got_row, got_col, got_cor, half_got, half_sum, quarter_send, quarter_got, total,
-    sino, msgs, inbox,
-    load_sem, rim_send, rim_recv, part_ssem, part_rsem, word_sem, a2a_send, a2a_recv, own_sem, out_sem,
+    sino_ref, row_ref, col_ref, cor_ref, part_ref, ramp_ref, bv_ref,
+    got_row, got_col, got_cor, total_out, inbox_out,
+    sino, part, ramp, bv, part_got, part_sum, quarter_send, quarter_got, total,
+    lines, over_send, over_got, msgs, inbox,
+    load_sem, rim_send, rim_recv, part_ssem, part_rsem, over_ssem, over_rsem,
+    word_sem, a2a_send, a2a_recv, own_sem, out_sem,
 ):
     ang, sy, sx = lax.axis_index("ang"), lax.axis_index("sy"), lax.axis_index("sx")
     oy, ox = 1 - sy, 1 - sx
     group = 2 * angles
     me = ang * 2 + sx
-    tile = sy * 2 + sx
 
     barrier = pltpu.get_barrier_semaphore()
-    steps = group.bit_length() - 1
-    partners = []
-    for r in range(steps):
-        d = jnp.bitwise_xor(me, 1 << r)
-        partners.append((d >> 1, sy, d & 1))
-    for dev in [(ang, oy, sx), (ang, oy, ox)] + partners:
+    line, place = ang >> 4, ang & 15
+    spot = line * 2 + sx
+    crosswise = []
+    for k in range(1, group // 16):
+        d = jnp.bitwise_xor(spot, k)
+        crosswise.append(((d >> 1) * 16 + place, sy, d & 1))
+    lengthwise = [(line * 16 + ((place + k) & 15), sy, sx) for k in range(1, 16)]
+    greeted = [(ang, oy, sx), (ang, oy, ox)] + crosswise + lengthwise
+    for dev in greeted:
         pl.semaphore_signal(barrier, inc=1, device_id=dev, device_id_type=MESH)
+    across, beside = (ang, oy, ox), (ang, sy, ox)
+    kind = jnp.bitwise_xor(sy, sx)
+    routes = (
+        (across, beside, 2 * sy, 2 * oy, sx, ox),
+        (beside, across, 2 * kind, 2 * (1 - kind), sy, oy),
+    )
     loads = [
         pltpu.make_async_copy(src, dst, load_sem.at[i])
         for i, (src, dst) in enumerate(
-            [(og_ref, og), (ramp_ref, ramp), (bv_ref, bv), (part_ref.at[pl.ds(2 * sy, 2)], part)]
+            [(sino_ref, sino), (ramp_ref, ramp), (bv_ref, bv)]
+            + [(part_ref.at[h, pl.ds(routes[h][2], 2)], part.at[h]) for h in range(2)]
         )
     ]
     for copy in loads:
         copy.start()
-    pl.semaphore_wait(barrier, steps + 2)
-
+    pl.semaphore_wait(barrier, len(greeted))
+
+    for dev in crosswise:
+        pl.semaphore_signal(word_sem, inc=1, device_id=dev, device_id_type=MESH)
+
+    def exchange(step, h, src, dst, dev):
+        return pltpu.make_async_remote_copy(
+            src_ref=src, dst_ref=dst, send_sem=part_ssem.at[step, h], recv_sem=part_rsem.at[step, h],
+            device_id=dev, device_id_type=MESH,
+        )
+
+    firsts = [
+        exchange(0, h, part_ref.at[h, pl.ds(routes[h][3], 2)], part_got.at[h], routes[h][0])
+        for h in range(2)
+    ]
+    for copy in firsts:
+        copy.start()
+    for copy in loads:
+        copy.wait()
+
+    for s in range(2):
+        filtered = jnp.dot(sino[...], ramp[s], preferred_element_type=F32).astype(BF)
+        lines[s] = jnp.dot(filtered, bv[s], preferred_element_type=F32)
+        for c in range(2):
+            over_send[s, c] = lines[s, 2 * TILE + c * RIM : 2 * TILE + (c + 1) * RIM, :].astype(BF)
+    over = pltpu.make_async_remote_copy(
+        src_ref=over_send, dst_ref=over_got, send_sem=over_ssem, recv_sem=over_rsem,
+        device_id=(ang, oy, sx), device_id_type=MESH,
+    )
+    over.start()
+    top = lax.broadcasted_iota(jnp.int32, (64, 8, BLK), 1) < 4
+    for s in range(2):
+        a = lines[s, 0:TILE, :].reshape(64, 8, BLK)
+        b = lines[s, TILE : 2 * TILE, :].reshape(64, 8, BLK)
+        lanes = slice(s * BLK, (s + 1) * BLK)
+        msgs[:, 0, :, lanes] = jnp.where(top, a, pltpu.roll(b, 4, 1)).astype(BF)
+        msgs[:, 1, :, lanes] = jnp.where(top, pltpu.roll(a, 4, 1), b).astype(BF)
+
+    def send_to(d):
+        @pl.when(d != me)
+        def _():
+            pltpu.make_async_remote_copy(
+                src_ref=msgs.at[d >> 1, d & 1], dst_ref=inbox.at[me],
+                send_sem=a2a_send, recv_sem=a2a_recv,
+                device_id=(d >> 1, sy, d & 1), device_id_type=MESH,
+            ).start()
+
+    inner = group - 16
+
+    def send_inner(k, carry):
+        send_to(16 * sy + lax.rem(me + k, inner))
+        return carry
+
+    def send_edge(k, carry):
+        send_to(inner * oy + ((me + k) & 15))
+        return carry
+
+    pl.semaphore_wait(word_sem, len(crosswise))
+    lax.fori_loop(0, inner // 2, send_inner, 0)
+    seconds = []
+    for h, (_, after, _, _, keep, give) in enumerate(routes):
+        firsts[h].wait()
+        part_sum[h] = part[h].astype(F32) + part_got[h].astype(F32)
+        quarter_send[h] = part_sum[h, give].astype(BF)
+        seconds.append(exchange(1, h, quarter_send.at[h], quarter_got.at[h], after))
+        seconds[h].start()
+    lax.fori_loop(inner // 2, inner, send_inner, 0)
+    over.wait()
+    edge = pl.ds(pl.multiple_of((TILE - RIM) * oy, RIM), RIM)
+    edge_low = pl.ds(pl.multiple_of(TILE + (TILE - RIM) * oy, RIM), RIM)
+    pairs = pl.ds(56 * oy, 8)
+    for s in range(2):
+        a = (lines[s, edge, :] + over_got[s, 0].astype(F32)).reshape(8, 8, BLK)
+        b = (lines[s, edge_low, :] + over_got[s, 1].astype(F32)).reshape(8, 8, BLK)
+        lanes = slice(s * BLK, (s + 1) * BLK)
+        msgs[pairs, 0, :, lanes] = jnp.where(top[0:8], a, pltpu.roll(b, 4, 1)).astype(BF)
+        msgs[pairs, 1, :, lanes] = jnp.where(top[0:8], pltpu.roll(a, 4, 1), b).astype(BF)
+    lax.fori_loop(0, 16, send_edge, 0)
+    own = pltpu.make_async_copy(msgs.at[ang, sx], inbox.at[me], own_sem)
+    own.start()
+
+    thirds = []
+    for h, (_, after, base, _, keep, _) in enumerate(routes):
+        seconds[h].wait()
+        at = total.at[h, base + keep]
+        total[h, base + keep] = (part_sum[h, keep] + quarter_got[h].astype(F32)).astype(BF)
+        thirds.append(exchange(2, h, at, at, after))
+        thirds[h].start()
     rims = [
         pltpu.make_async_remote_copy(
             src_ref=src, dst_ref=dst, send_sem=rim_send.at[i], recv_sem=rim_recv.at[i],
@@ -325,130 +432,82 @@
         for i, (src, dst, dev) in enumerate(
             [
                 (row_ref, got_row, (ang, oy, sx)),
-                (col_ref, got_col, (ang, sy, ox)),
-                (cor_ref, got_cor, (ang, oy, ox)),
+                (col_ref, got_col, beside),
+                (cor_ref, got_cor, across),
             ]
         )
     ]
     for copy in rims:
         copy.start()
-    def exchange(i, src, dst, dev):
-        return pltpu.make_async_remote_copy(
-            src_ref=src, dst_ref=dst, send_sem=part_ssem.at[i], recv_sem=part_rsem.at[i],
-            device_id=dev, device_id_type=MESH,
-        )
-
-    across, beside = (ang, oy, ox), (ang, sy, ox)
-    halves = exchange(0, part_ref.at[pl.ds(2 * oy, 2)], half_got, across)
-    halves.start()
-    for copy in loads:
-        copy.wait()
-    for r in range(steps):
-        pl.semaphore_signal(word_sem.at[r], inc=1, device_id=partners[r], device_id_type=MESH)
-        pl.semaphore_wait(word_sem.at[r], 1)
-    for copy in rims:
-        copy.wait()
-    halves.wait()
-    half_sum[...] = part[...].astype(F32) + half_got[...].astype(F32)
-    quarter_send[...] = half_sum[ox].astype(BF)
-    quarters = exchange(1, quarter_send, quarter_got, beside)
-    quarters.start()
-    row_at = pl.ds(pl.multiple_of((TILE - RIM) * oy, RIM), RIM)
-    col_at = pl.ds(pl.multiple_of((TILE - BLK) * ox, BLK), BLK)
-    for c in range(2):
-        og[c, row_at, :] = og[c, row_at, :] + got_row[c].astype(F32)
-    first = lax.broadcasted_iota(jnp.int32, (TILE, BLK), 1) < RIM
-    for got, at in ((got_col, pl.ds(0, TILE)), (got_cor, row_at)):
-        wide = got[...].astype(F32)
-        turned = swap_halves(wide)
-        low = first[: wide.shape[0]]
-        added = (
-            jnp.where(sx == 1, jnp.where(low, wide, 0.0), jnp.where(low, 0.0, turned)),
-            jnp.where(sx == 1, jnp.where(low, turned, 0.0), jnp.where(low, 0.0, wide)),
-        )
-        for c in range(2):
-            og[c, at, col_at] = og[c, at, col_at] + added[c]
-    og_copy = pltpu.make_async_copy(og, og_out, out_sem.at[0])
-    og_copy.start()
-
-    sino[...] = og[...].astype(BF).reshape(2 * TILE, TILE)
-    lines = []
-    for s in range(2):
-        filtered = jnp.dot(sino[...], ramp[s], preferred_element_type=F32).astype(BF)
-        lines.append(jnp.dot(filtered, bv[s], preferred_element_type=F32))
-    top = lax.broadcasted_iota(jnp.int32, (64, 8, BLK), 1) < 4
-    for s in range(2):
-        a = lines[s][0:TILE].reshape(64, 8, BLK)
-        b = lines[s][TILE:].reshape(64, 8, BLK)
-        lanes = slice(s * BLK, (s + 1) * BLK)
-        msgs[:, 0, :, lanes] = jnp.where(top, a, pltpu.roll(b, 4, 1)).astype(BF)
-        msgs[:, 1, :, lanes] = jnp.where(top, pltpu.roll(a, 4, 1), b).astype(BF)
-
-    def send(k, carry):
-        d = lax.rem(me + k, group)
-        pltpu.make_async_remote_copy(
-            src_ref=msgs.at[d // 2, lax.rem(d, 2)], dst_ref=inbox.at[me],
-            send_sem=a2a_send, recv_sem=a2a_recv,
-            device_id=(d // 2, sy, lax.rem(d, 2)), device_id_type=MESH,
-        ).start()
-        return carry
-
-    lax.fori_loop(1, group, send, 0)
-    own = pltpu.make_async_copy(msgs.at[ang, sx], inbox.at[me], own_sem)
-    own.start()
-
-    quarters.wait()
-    total[tile] = (half_sum[sx] + quarter_got[...].astype(F32)).astype(BF)
-    shared = exchange(2, total.at[tile], total.at[tile], beside)
-    shared.start()
-    shared.wait()
-    mine = pl.ds(2 * sy, 2)
-    rest = exchange(3, total.at[mine], total.at[mine], across)
-    rest.start()
+    fourths = []
+    for h, (before, _, base, _, _, _) in enumerate(routes):
+        thirds[h].wait()
+        at = total.at[h, pl.ds(base, 2)]
+        fourths.append(exchange(3, h, at, at, before))
+        fourths[h].start()
     own.wait()
     pltpu.make_async_copy(
         inbox.at[pl.ds(0, group - 1)], inbox.at[pl.ds(0, group - 1)], a2a_recv
     ).wait()
-    inbox_copy = pltpu.make_async_copy(inbox, inbox_out, out_sem.at[1])
+    inbox_copy = pltpu.make_async_copy(inbox, inbox_out, out_sem.at[0])
     inbox_copy.start()
-    rest.wait()
-    total_copy = pltpu.make_async_copy(total, total_out, out_sem.at[2])
+    for copy in fourths:
+        copy.wait()
+    total_copy = pltpu.make_async_copy(total, total_out, out_sem.at[1])
     total_copy.start()
     pltpu.make_async_copy(
         inbox.at[pl.ds(0, group - 1)], inbox.at[pl.ds(0, group - 1)], a2a_send
     ).wait()
-    og_copy.wait()
+    for copy in rims:
+        copy.wait()
     inbox_copy.wait()
     total_copy.wait()
 
 
 def finish_kernel(
-    angles, bi_ref, og_ref, total_ref, inbox_ref, og_out, pg_out, vol_out,
-    og, total, pg, inbox, vol, seen, in_sem, og_sem, out_sem,
+    angles, bi_ref, og_ref, row_ref, col_ref, cor_ref, total_ref, inbox_ref, og_out, pg_out, vol_out,
+    og, row, col, cor, total, pg, inbox, vol, seen, in_sem, out_sem,
 ):
-    arrived = pltpu.make_async_copy(inbox_ref, inbox, in_sem.at[0])
-    summed = pltpu.make_async_copy(total_ref, total, in_sem.at[1])
-    arrived.start()
-    summed.start()
-    pieces = [
-        (
-            pltpu.make_async_copy(og_ref.at[:, pl.ds(i * 128, 128)], og.at[:, pl.ds(i * 128, 128)], og_sem.at[i]),
-            pltpu.make_async_copy(og.at[:, pl.ds(i * 128, 128)], og_out.at[0, :, pl.ds(i * 128, 128)], og_sem.at[i + 4]),
-        )
-        for i in range(4)
+    sy, sx = lax.axis_index("sy"), lax.axis_index("sx")
+    oy, ox = 1 - sy, 1 - sx
+    loads = [
+        pltpu.make_async_copy(src, dst, in_sem.at[i])
+        for i, (src, dst) in enumerate(
+            [
+                (og_ref, og), (row_ref, row), (col_ref, col), (cor_ref, cor),
+                (total_ref, total), (inbox_ref, inbox),
+            ]
+        )
     ]
-    for load, _ in pieces:
-        load.start()
+    for copy in loads:
+        copy.start()
+    summed, arrived = loads[4:]
     for a in range(angles):
         seen[a] = 0
     summed.wait()
     for q in range(4):
-        pg[0, q // 2, q % 2] = total[q].astype(F32) * (1.0 / math.sqrt(8.0))
+        pg[0, q // 2, q % 2, 0:BLK, :] = total[0, q].astype(F32) * (1.0 / math.sqrt(8.0))
+        pg[0, q // 2, q % 2, BLK:, :] = total[1, SECOND[q]].astype(F32) * (1.0 / math.sqrt(8.0))
     pg_copy = pltpu.make_async_copy(pg, pg_out, out_sem.at[0])
     pg_copy.start()
-    for load, store in pieces:
-        load.wait()
-        store.start()
+    for copy in loads[0:4]:
+        copy.wait()
+    row_at = pl.ds(pl.multiple_of((TILE - RIM) * oy, RIM), RIM)
+    col_at = pl.ds(pl.multiple_of((TILE - BLK) * ox, BLK), BLK)
+    for got, at in ((col, pl.ds(0, TILE)), (cor, row_at)):
+        wide = got[...].astype(F32)
+        turned = swap_halves(wide)
+        low = lax.broadcasted_iota(jnp.int32, wide.shape, 1) < RIM
+        added = (
+            jnp.where(sx == 1, jnp.where(low, wide, 0.0), jnp.where(low, 0.0, turned)),
+            jnp.where(sx == 1, jnp.where(low, turned, 0.0), jnp.where(low, 0.0, wide)),
+        )
+        for c in range(2):
+            og[c, at, col_at] = og[c, at, col_at] + added[c]
+    for c in range(2):
+        og[c, row_at, :] = og[c, row_at, :] + row[c].astype(F32)
+    og_copy = pltpu.make_async_copy(og, og_out.at[0], out_sem.at[2])
+    og_copy.start()
     arrived.wait()
     for b in range(8):
         line = jnp.zeros((8, BLK), F32)
@@ -464,8 +523,7 @@
                 vol[0, r, c, b * BLK : (b + 1) * BLK] = line[c * 4 + r]
     vol_copy = pltpu.make_async_copy(vol, vol_out, out_sem.at[1])
     vol_copy.start()
-    for _, store in pieces:
-        store.wait()
+    og_copy.wait()
     pg_copy.wait()
     vol_copy.wait()
 
@@ -493,13 +551,14 @@
             collective_id=0, has_side_effects=True, vmem_limit_bytes=62 * 1024 * 1024
         ),
     )(objects)
-    og_part, row, col, cor, parts, ramp_two, bv_two = pl.pallas_call(
+    og_part, row, col, cor, parts, ramp_two, bv_two, sino = pl.pallas_call(
         functools.partial(patch_kernel, angles),
         out_shape=(shape((2, TILE, TILE), F32),) + rim_shapes + (
-            shape((4, PATCH, PATCH), BF), shape((2, TILE, BLK), BF), shape((2, BLK, BLK), BF),
+            shape((2, 4, BLK, PATCH), BF), shape((2, SPAN, BLK), BF), shape((2, BLK, BLK), BF),
+            shape((2 * ROWS - 2 * RIM, SPAN), BF),
         ),
         in_specs=[smem] * 2 + [hbm] * 10,
-        out_specs=[hbm] * 7,
+        out_specs=[hbm] * 8,
         scratch_shapes=[
             pltpu.VMEM((2, ROWS, COLS), BF),
             pltpu.VMEM((ROWS, BLK), BF),
@@ -507,7 +566,7 @@
             pltpu.VMEM((2, PATCH, PATCH), BF),
             pltpu.VMEM((512, 512), BF),
             pltpu.VMEM((512, 512), BF),
-            pltpu.VMEM((2, TILE, BLK), BF),
+            pltpu.VMEM((2, SPAN, BLK), BF),
             pltpu.VMEM((2, BLK, BLK), BF),
             pltpu.VMEM((2, 2, 272, BLK), F32),
             pltpu.VMEM((2, 2, PATCH, PATCH), F32),
@@ -520,59 +579,60 @@
             pltpu.VMEM((2, RIM, TILE), BF),
             pltpu.VMEM((TILE, BLK), BF),
             pltpu.VMEM((RIM, BLK), BF),
-            pltpu.VMEM((4, PATCH, PATCH), BF),
-            dma((8,)), dma((4,)), dma((7,)),
+            pltpu.VMEM((2, 4, BLK, PATCH), BF),
+            pltpu.VMEM((2 * ROWS - 2 * RIM, SPAN), BF),
+            dma((8,)), dma((4,)), dma((8,)),
         ],
         compiler_params=pltpu.CompilerParams(vmem_limit_bytes=62 * 1024 * 1024),
     )(positions, block_index, objects, *halos, probe, data, forward, backward, ramp, block_values)
-    og, total, inbox = pl.pallas_call(
+    got_row, got_col, got_cor, total, inbox = pl.pallas_call(
         functools.partial(regroup_kernel, angles),
-        out_shape=(
-            shape((2, TILE, TILE), F32), shape((4, PATCH, PATCH), BF), shape((group, 8, 2 * BLK), BF),
-        ),
+        out_shape=rim_shapes + (shape((2, 4, BLK, PATCH), BF), shape((group, 8, 2 * BLK), BF)),
         in_specs=[hbm] * 7,
-        out_specs=[hbm] * 3,
+        out_specs=[hbm] * 5,
         scratch_shapes=[
-            pltpu.VMEM((2, TILE, TILE), F32),
-            pltpu.VMEM((2, PATCH, PATCH), BF),
-            pltpu.VMEM((2, TILE, BLK), BF),
+            pltpu.VMEM((2 * ROWS - 2 * RIM, SPAN), BF),
+            pltpu.VMEM((2, 2, BLK, PATCH), BF),
+            pltpu.VMEM((2, SPAN, BLK), BF),
             pltpu.VMEM((2, BLK, BLK), BF),
-            pltpu.VMEM((2, RIM, TILE), BF),
-            pltpu.VMEM((TILE, BLK), BF),
-            pltpu.VMEM((RIM, BLK), BF),
-            pltpu.VMEM((2, PATCH, PATCH), BF),
-            pltpu.VMEM((2, PATCH, PATCH), F32),
-            pltpu.VMEM((PATCH, PATCH), BF),
-            pltpu.VMEM((PATCH, PATCH), BF),
-            pltpu.VMEM((4, PATCH, PATCH), BF),
-            pltpu.VMEM((2 * TILE, TILE), BF),
+            pltpu.VMEM((2, 2, BLK, PATCH), BF),
+            pltpu.VMEM((2, 2, BLK, PATCH), F32),
+            pltpu.VMEM((2, BLK, PATCH), BF),
+            pltpu.VMEM((2, BLK, PATCH), BF),
+            pltpu.VMEM((2, 4, BLK, PATCH), BF),
+            pltpu.VMEM((2, 2 * ROWS - 2 * RIM, BLK), F32),
+            pltpu.VMEM((2, 2, RIM, BLK), BF),
+            pltpu.VMEM((2, 2, RIM, BLK), BF),
             pltpu.VMEM((group // 2, 2, 8, 2 * BLK), BF),
             pltpu.VMEM((group, 8, 2 * BLK), BF),
-            dma((4,)), dma((3,)), dma((3,)), dma((4,)), dma((4,)),
-            pltpu.SemaphoreType.REGULAR((group.bit_length() - 1,)), dma, dma, dma, dma((3,)),
+            dma((5,)), dma((3,)), dma((3,)), dma((4, 2)), dma((4, 2)), dma, dma,
+            pltpu.SemaphoreType.REGULAR, dma, dma, dma, dma((2,)),
         ],
         compiler_params=pltpu.CompilerParams(
             collective_id=1, has_side_effects=True, vmem_limit_bytes=62 * 1024 * 1024
         ),
-    )(og_part, row, col, cor, parts, ramp_two, bv_two)
+    )(sino, row, col, cor, parts, ramp_two, bv_two)
     return pl.pallas_call(
         functools.partial(finish_kernel, angles),
         out_shape=(
             shape((1, 2, TILE, TILE), F32), shape((1, 2, 2, PATCH, PATCH), F32), shape((1, 4, 2, 1024), F32),
         ),
-        in_specs=[smem] + [hbm] * 3,
+        in_specs=[smem] + [hbm] * 6,
         out_specs=[hbm] * 3,
         scratch_shapes=[
             pltpu.VMEM((2, TILE, TILE), F32),
-            pltpu.VMEM((4, PATCH, PATCH), BF),
+            pltpu.VMEM((2, RIM, TILE), BF),
+            pltpu.VMEM((TILE, BLK), BF),
+            pltpu.VMEM((RIM, BLK), BF),
+            pltpu.VMEM((2, 4, BLK, PATCH), BF),
             pltpu.VMEM((1, 2, 2, PATCH, PATCH), F32),
             pltpu.VMEM((group, 8, 2 * BLK), BF),
             pltpu.VMEM((1, 4, 2, 1024), F32),
             pltpu.SMEM((angles,), jnp.int32),
-            dma((2,)), dma((8,)), dma((2,)),
+            dma((6,)), dma((3,)),
         ],
         compiler_params=pltpu.CompilerParams(vmem_limit_bytes=62 * 1024 * 1024),
-    )(block_index, og, total, inbox)
+    )(block_index, og_part, got_row, got_col, got_cor, total, inbox)
 
 
 def solution(mesh):

time: 62.8 us -> 59.8 us (0.952)
  Pallas kernels: 61.7 us -> 59 us
    pallas_call x1, Pallas kernels: 36.7 us -> 33 us  [body(): pl.pallas_call(functools.partial(regroup_kernel, angles), out_shape=rim_s...]
    pallas_call x1, Pallas kernels: 10.3 us -> 11.3 us  [body(): pl.pallas_call(functools.partial(patch_kernel, angles), out_shape=(shape(...]
where the time goes in v3:
time: 59.8 us; the launch traced here: 59.6 us
  Pallas kernels  59 us (99%)
  between operations  0.65 us (1%)
    pallas_call x1, Pallas kernels, body(): pl.pallas_call(functools.partial(regroup_kernel, angles), out_shape=rim_s...  33 us
    pallas_call x1, Pallas kernels, body(): pl.pallas_call(functools.partial(patch_kernel, angles), out_shape=(shape(...  11.3 us
    pallas_call x1, Pallas kernels, body(): pl.pallas_call(strips_kernel, out_shape=rim_shapes, in_specs=[hbm], out_s...  10.4 us
    pallas_call x1, Pallas kernels, body(): pl.pallas_call(functools.partial(finish_kernel, angles), out_shape=(shape...  4.32 us

profile of v3, /device:TPU:1, one launch (start us, length us, event | category | flops | bytes accessed | tf_op | source)
XLA Modules:
  0.0 59.6 jit_solution(15655269302390590947)
XLA Ops:
  0.6 10.4 %shard_map.112 = (bf16[2,64,512]{2,1,0:T(8,128)(2,1)}, bf16[512,128]{1,0:T(8,128)(2,1)}, bf16[64,128]{1,0:T(8,128)(2,1)}) custom-call(bf16[1,2,512,512]{3,2,1,0:T(8,128)(2,1)} %obj_ref.3), custom_call_target="tpu_custom_call" | custom-call | tf_op jit(solution)/shard_map/pallas_call | solution.py:542
  11.0 11.3 %shard_map.113 = (f32[2,512,512]{2,1,0:T(8,128)}, bf16[2,64,512]{2,1,0:T(8,128)(2,1)}, bf16[512,128]{1,0:T(8,128)(2,1)}, bf16[64,128]{1,0:T(8,128)(2,1)}, bf16[2...) custom-call(s32[1,1,1,2,2]{4,3,2,1,0:T(2,128)} %pos_ref.1, ...), custom_call_target="tpu_custom_call" | custom-call | tf_op jit(solution)/shard_map/pallas_call | solution.py:554
  22.3 33.0 %shard_map.114 = (bf16[2,64,512]{2,1,0:T(8,128)(2,1)}, bf16[512,128]{1,0:T(8,128)(2,1)}, bf16[64,128]{1,0:T(8,128)(2,1)}, bf16[2,4,128,256]{3,2,1,0:T(8,128)(2,1)}, bf16[128,8,256]{2,1,0:T(8,128)(2,1)}) custom-call(bf16[1152,640]{1,0:T(8,128)(2,1)} %get-tuple-element.23.sino_ref, bf16[2,64,512]{2,1,0:T(8,128)(2,1)} %get-tuple-element.24.row_ref, ...), custom_call_target="tpu_custom_call" | custom-call | tf_op jit(solution)/shard_map/pallas_call | solution.py:588
  55.3 4.3 %shard_map.115 = (f32[1,2,512,512]{3,2,1,0:T(8,128)}, f32[1,2,2,256,256]{4,3,2,1,0:T(8,128)}, f32[1,4,2,1024]{3,2,1,0:T(2,128)}) custom-call(s32[8,16]{1,0:T(8,128)} %bi_ref.3, f32[2,512,512]{2,1,0:T(8,128)} %get-tuple-element.22.og_ref, bf16[2,64,512]{2,1,0:T(8,128)(2,1)} %get-tuple-element.30.row_ref, bf16[512,128]{1,0:T(8,128)(2,1)} %get-tuple-element.31.col_ref, ...), custom_call_target="tpu_custom_call" | custom-call | tf_op jit(solution)/shard_map/pallas_call | solution.py:615

commit v4 on v3

--- a/solution.py
+++ b/solution.py
@@ -47,7 +47,9 @@
     return pltpu.roll(cells, BLK // 2, cells.ndim - 1)
 
 
-def strips_kernel(obj_ref, row_out, col_out, cor_out, block, packed, load_sem, send_sem, recv_sem):
+def strips_kernel(
+    angles, bi_ref, obj_ref, named_out, row_out, col_out, cor_out, block, packed, load_sem, send_sem, recv_sem,
+):
     ang, sy, sx = lax.axis_index("ang"), lax.axis_index("sy"), lax.axis_index("sx")
     oy, ox = 1 - sy, 1 - sx
     devices = [(ang, oy, sx), (ang, sy, ox), (ang, oy, ox)]
@@ -75,19 +77,32 @@
     ]
     for copy in copies:
         copy.start()
+    named = [(jnp.int32(-1), jnp.int32(0)), (jnp.int32(0), jnp.int32(0))]
+    for j in range(2 * angles):
+        entry = bi_ref[j // 16, j % 16]
+        mine = (entry >> 3) == ang
+        early = jnp.logical_and(mine, named[0][0] < 0)
+        named = [
+            (jnp.where(take, j, at), jnp.where(take, entry & 7, column))
+            for take, (at, column) in zip((early, mine), named)
+        ]
+    named[0] = (jnp.maximum(named[0][0], 0), named[0][1])
+    for s, (entry, column) in enumerate(named):
+        named_out[2 * s] = entry
+        named_out[2 * s + 1] = column
     for copy in copies:
         copy.wait()
 
 
 def patch_kernel(
     angles,
-    pos_ref, bi_ref,
+    pos_ref, named_ref,
     obj_ref, halo_row, halo_col, halo_cor, probe_ref, data_ref, fwd_ref, bwd_ref, ramp_ref, bv_ref,
     og_out, row_out, col_out, cor_out, part_out, ramp_out, bv_out, sino_out,
     big, side, probe, data, fwd, bwd, ramp, bv,
     win, patch, exits, half, far, chi, placed, og,
     rim_row, rim_col, rim_cor, part, sino,
-    load_sem, pick_sem, out_sem,
+    load_sem, pick_sem, out_sem, piece_sem,
 ):
     ang, sy, sx = lax.axis_index("ang"), lax.axis_index("sy"), lax.axis_index("sx")
     oy, ox = 1 - sy, 1 - sx
@@ -119,16 +134,7 @@
         placed[q, 0, RIM : RIM + PATCH, :] = jnp.zeros((PATCH, BLK), F32)
         placed[q, 4, RIM : RIM + PATCH, :] = jnp.zeros((PATCH, BLK), F32)
 
-    named = [(jnp.int32(-1), jnp.int32(0)), (jnp.int32(0), jnp.int32(0))]
-    for j in range(2 * angles):
-        entry = bi_ref[j // 16, j % 16]
-        mine = (entry >> 3) == ang
-        early = jnp.logical_and(mine, named[0][0] < 0)
-        named = [
-            (jnp.where(take, j, at), jnp.where(take, entry & 7, column))
-            for take, (at, column) in zip((early, mine), named)
-        ]
-    named[0] = (jnp.maximum(named[0][0], 0), named[0][1])
+    named = [(named_ref[0], named_ref[1]), (named_ref[2], named_ref[3])]
     picks = []
     for s, (entry, column) in enumerate(named):
         at = pl.multiple_of((7 - column + 3 * sx) * BLK, BLK)
@@ -141,7 +147,7 @@
     for copy in picks:
         copy.start()
     side[pl.ds(pl.multiple_of((ROWS - RIM) * sy, RIM), RIM), :] = jnp.zeros((RIM, BLK), BF)
-    for copy in loads:
+    for copy in loads[0:4]:
         copy.wait()
     wide = side[...].astype(F32)
     turned = swap_halves(wide)
@@ -170,13 +176,29 @@
         for c in range(2):
             for b in range(2):
                 patch[p, c, :, b * BLK : (b + 1) * BLK] = win[c, b, pl.ds(lead, PATCH), :]
+        @pl.when(p == 0)
+        def _():
+            loads[4].wait()
+
         for m in range(2):
             exits[m, 0:PATCH] = (probe[m, 0] * patch[p, 0] - probe[m, 1] * patch[p, 1]).astype(BF)
             exits[m, PATCH:] = (probe[m, 0] * patch[p, 1] + probe[m, 1] * patch[p, 0]).astype(BF)
+        @pl.when(p == 0)
+        def _():
+            loads[5].wait()
+
         for m in range(2):
             done = jnp.dot(fwd[...], exits[m], preferred_element_type=F32)
             half[m, :, 0:PATCH] = done[0:PATCH].astype(BF)
             half[m, :, PATCH:] = done[PATCH:].astype(BF)
+        @pl.when(p == 0)
+        def _():
+            loads[6].wait()
+
+        @pl.when(p == 0)
+        def _():
+            loads[7].wait()
+
         for m in range(2):
             far[m] = jnp.dot(half[m], bwd[...], preferred_element_type=F32)
         misfit = (
@@ -250,7 +272,7 @@
         for i, (src, dst) in enumerate(
             [
                 (rim_row, row_out), (rim_col, col_out), (rim_cor, cor_out),
-                (og, og_out), (part, part_out), (ramp, ramp_out), (bv, bv_out), (sino, sino_out),
+                (part, part_out), (ramp, ramp_out), (bv, bv_out),
             ]
         )
     ]
@@ -258,7 +280,7 @@
         copy.start()
     for copy in picks:
         copy.wait()
-    for copy in outs[5:7]:
+    for copy in outs[4:6]:
         copy.start()
 
     for c in range(2):
@@ -266,6 +288,18 @@
             sino[2 * TILE + c * RIM : 2 * TILE + (c + 1) * RIM, b * BLK : (b + 1) * BLK] = cells_at(
                 c, rim_chunk, b + ox
             ).astype(BF)
+
+    over_rows = pl.ds(2 * TILE, 2 * RIM)
+    over_copy = pltpu.make_async_copy(sino.at[over_rows], sino_out.at[over_rows], out_sem.at[6])
+    over_copy.start()
+
+    def finished(r):
+        rows = pl.ds(pl.multiple_of(r * RIM, RIM), RIM)
+        spans = [pl.ds(pl.multiple_of(c * TILE + r * RIM, RIM), RIM) for c in range(2)]
+        return [pltpu.make_async_copy(og.at[:, rows], og_out.at[0, :, rows], piece_sem.at[r, 2])] + [
+            pltpu.make_async_copy(sino.at[spans[c]], sino_out.at[spans[c]], piece_sem.at[r, c])
+            for c in range(2)
+        ]
 
     def interior(r, carry):
         rows = pl.ds(pl.multiple_of(r * RIM, RIM), RIM)
@@ -276,11 +310,11 @@
                 sino[pl.ds(pl.multiple_of(c * TILE + r * RIM, RIM), RIM), b * BLK : (b + 1) * BLK] = cells_at(
                     c, r + 1, b + ox
                 ).astype(BF)
+        for copy in finished(r):
+            copy.start()
         return carry
 
     lax.fori_loop(0, 8, interior, 0)
-    outs[7].start()
-    outs[3].start()
 
     for m in range(2):
         real, imag = (
@@ -291,9 +325,17 @@
         for q, terms in ((2 * m, real), (2 * m + 1, imag)):
             part[0, q] = terms[0:BLK].astype(BF)
             part[1, SECOND[q]] = terms[BLK:].astype(BF)
-    outs[4].start()
+    outs[3].start()
+
+    def settle(r, carry):
+        for copy in finished(r):
+            copy.wait()
+        return carry
+
+    lax.fori_loop(0, 8, settle, 0)
     for copy in outs:
         copy.wait()
+    over_copy.wait()
 
 
 def regroup_kernel(
@@ -466,22 +508,25 @@
 
 def finish_kernel(
     angles, bi_ref, og_ref, row_ref, col_ref, cor_ref, total_ref, inbox_ref, og_out, pg_out, vol_out,
-    og, row, col, cor, total, pg, inbox, vol, seen, in_sem, out_sem,
+    og_row, og_col, row, col, cor, total, pg, inbox, vol, seen, in_sem, out_sem,
 ):
     sy, sx = lax.axis_index("sy"), lax.axis_index("sx")
     oy, ox = 1 - sy, 1 - sx
+    row_at = pl.ds(pl.multiple_of((TILE - RIM) * oy, RIM), RIM)
+    col_at = pl.ds(pl.multiple_of((TILE - BLK) * ox, BLK), BLK)
+    rest_at = pl.ds(pl.multiple_of(BLK * sx, BLK), TILE - BLK)
     loads = [
         pltpu.make_async_copy(src, dst, in_sem.at[i])
         for i, (src, dst) in enumerate(
             [
-                (og_ref, og), (row_ref, row), (col_ref, col), (cor_ref, cor),
-                (total_ref, total), (inbox_ref, inbox),
+                (og_ref.at[0, :, row_at, rest_at], og_row), (og_ref.at[0, :, :, col_at], og_col),
+                (row_ref, row), (col_ref, col), (cor_ref, cor), (total_ref, total), (inbox_ref, inbox),
             ]
         )
     ]
     for copy in loads:
         copy.start()
-    summed, arrived = loads[4:]
+    summed, arrived = loads[5:]
     for a in range(angles):
         seen[a] = 0
     summed.wait()
@@ -490,10 +535,8 @@
         pg[0, q // 2, q % 2, BLK:, :] = total[1, SECOND[q]].astype(F32) * (1.0 / math.sqrt(8.0))
     pg_copy = pltpu.make_async_copy(pg, pg_out, out_sem.at[0])
     pg_copy.start()
-    for copy in loads[0:4]:
-        copy.wait()
-    row_at = pl.ds(pl.multiple_of((TILE - RIM) * oy, RIM), RIM)
-    col_at = pl.ds(pl.multiple_of((TILE - BLK) * ox, BLK), BLK)
+    for copy in loads[0:5]:
+        copy.wait()
     for got, at in ((col, pl.ds(0, TILE)), (cor, row_at)):
         wide = got[...].astype(F32)
         turned = swap_halves(wide)
@@ -503,11 +546,16 @@
             jnp.where(sx == 1, jnp.where(low, turned, 0.0), jnp.where(low, 0.0, wide)),
         )
         for c in range(2):
-            og[c, at, col_at] = og[c, at, col_at] + added[c]
+            og_col[c, at, :] = og_col[c, at, :] + added[c]
     for c in range(2):
-        og[c, row_at, :] = og[c, row_at, :] + row[c].astype(F32)
-    og_copy = pltpu.make_async_copy(og, og_out.at[0], out_sem.at[2])
-    og_copy.start()
+        og_row[c] = og_row[c] + row[c, :, rest_at].astype(F32)
+        og_col[c, row_at, :] = og_col[c, row_at, :] + row[c, :, col_at].astype(F32)
+    og_copies = [
+        pltpu.make_async_copy(og_row, og_out.at[0, :, row_at, rest_at], out_sem.at[2]),
+        pltpu.make_async_copy(og_col, og_out.at[0, :, :, col_at], out_sem.at[3]),
+    ]
+    for copy in og_copies:
+        copy.start()
     arrived.wait()
     for b in range(8):
         line = jnp.zeros((8, BLK), F32)
@@ -523,7 +571,8 @@
                 vol[0, r, c, b * BLK : (b + 1) * BLK] = line[c * 4 + r]
     vol_copy = pltpu.make_async_copy(vol, vol_out, out_sem.at[1])
     vol_copy.start()
-    og_copy.wait()
+    for copy in og_copies:
+        copy.wait()
     pg_copy.wait()
     vol_copy.wait()
 
@@ -539,21 +588,21 @@
         return jax.ShapeDtypeStruct(dims, kind)
 
     rim_shapes = (shape((2, RIM, TILE), BF), shape((TILE, BLK), BF), shape((RIM, BLK), BF))
-    halos = pl.pallas_call(
-        strips_kernel,
-        out_shape=rim_shapes,
-        in_specs=[hbm],
-        out_specs=[hbm] * 3,
+    named, *halos = pl.pallas_call(
+        functools.partial(strips_kernel, angles),
+        out_shape=(shape((4,), jnp.int32),) + rim_shapes,
+        in_specs=[smem, hbm],
+        out_specs=[smem] + [hbm] * 3,
         scratch_shapes=[
             pltpu.VMEM((2, TILE, BLK), BF), pltpu.VMEM((TILE, BLK), BF), dma, dma((3,)), dma((3,)),
         ],
         compiler_params=pltpu.CompilerParams(
             collective_id=0, has_side_effects=True, vmem_limit_bytes=62 * 1024 * 1024
         ),
-    )(objects)
+    )(block_index, objects)
     og_part, row, col, cor, parts, ramp_two, bv_two, sino = pl.pallas_call(
         functools.partial(patch_kernel, angles),
-        out_shape=(shape((2, TILE, TILE), F32),) + rim_shapes + (
+        out_shape=(shape((1, 2, TILE, TILE), F32),) + rim_shapes + (
             shape((2, 4, BLK, PATCH), BF), shape((2, SPAN, BLK), BF), shape((2, BLK, BLK), BF),
             shape((2 * ROWS - 2 * RIM, SPAN), BF),
         ),
@@ -581,10 +630,10 @@
             pltpu.VMEM((RIM, BLK), BF),
             pltpu.VMEM((2, 4, BLK, PATCH), BF),
             pltpu.VMEM((2 * ROWS - 2 * RIM, SPAN), BF),
-            dma((8,)), dma((4,)), dma((8,)),
+            dma((8,)), dma((4,)), dma((7,)), dma((8, 3)),
         ],
         compiler_params=pltpu.CompilerParams(vmem_limit_bytes=62 * 1024 * 1024),
-    )(positions, block_index, objects, *halos, probe, data, forward, backward, ramp, block_values)
+    )(positions, named, objects, *halos, probe, data, forward, backward, ramp, block_values)
     got_row, got_col, got_cor, total, inbox = pl.pallas_call(
         functools.partial(regroup_kernel, angles),
         out_shape=rim_shapes + (shape((2, 4, BLK, PATCH), BF), shape((group, 8, 2 * BLK), BF)),
@@ -620,7 +669,8 @@
         in_specs=[smem] + [hbm] * 6,
         out_specs=[hbm] * 3,
         scratch_shapes=[
-            pltpu.VMEM((2, TILE, TILE), F32),
+            pltpu.VMEM((2, RIM, TILE - BLK), F32),
+            pltpu.VMEM((2, TILE, BLK), F32),
             pltpu.VMEM((2, RIM, TILE), BF),
             pltpu.VMEM((TILE, BLK), BF),
             pltpu.VMEM((RIM, BLK), BF),
@@ -629,8 +679,9 @@
             pltpu.VMEM((group, 8, 2 * BLK), BF),
             pltpu.VMEM((1, 4, 2, 1024), F32),
             pltpu.SMEM((angles,), jnp.int32),
-            dma((6,)), dma((3,)),
+            dma((7,)), dma((4,)),
         ],
+        input_output_aliases={1: 0},
         compiler_params=pltpu.CompilerParams(vmem_limit_bytes=62 * 1024 * 1024),
     )(block_index, og_part, got_row, got_col, got_cor, total, inbox)
 

time: 59.8 us -> 59.2 us (0.990)
  Pallas kernels: 59 us -> 58.3 us
    pallas_call x1, Pallas kernels: 10.4 us -> 11.6 us  [body(): pl.pallas_call(functools.partial(strips_kernel, angles), out_shape=(shape...]
    pallas_call x1, Pallas kernels: 11.3 us -> 10.4 us  [body(): pl.pallas_call(functools.partial(patch_kernel, angles), out_shape=(shape(...]
    pallas_call x1, Pallas kernels: 4.32 us -> 3.54 us  [body(): pl.pallas_call(functools.partial(finish_kernel, angles), out_shape=(shape...]
where the time goes in v4:
time: 59.2 us; the launch traced here: 58.9 us
  Pallas kernels  58.3 us (98%)
  between operations  0.65 us (1%)
    pallas_call x1, Pallas kernels, body(): pl.pallas_call(functools.partial(regroup_kernel, angles), out_shape=rim_s...  32.7 us
    pallas_call x1, Pallas kernels, body(): pl.pallas_call(functools.partial(strips_kernel, angles), out_shape=(shape...  11.6 us
    pallas_call x1, Pallas kernels, body(): pl.pallas_call(functools.partial(patch_kernel, angles), out_shape=(shape(...  10.4 us
    pallas_call x1, Pallas kernels, body(): pl.pallas_call(functools.partial(finish_kernel, angles), out_shape=(shape...  3.54 us

profile of v4, /device:TPU:1, one launch (start us, length us, event | category | flops | bytes accessed | tf_op | source)
XLA Modules:
  0.0 58.9 jit_solution(1063693301735833941)
XLA Ops:
  0.6 11.6 %shard_map.112 = (s32[4]{0:T(128)}, bf16[2,64,512]{2,1,0:T(8,128)(2,1)}, bf16[512,128]{1,0:T(8,128)(2,1)}, bf16[64,128]{1,0:T(8,128)(2,1)}) custom-call(s32[8,16]{1,0:T(8,128)} %bi_ref.3, bf16[1,2,512,512]{3,2,1,0:T(8,128)(2,1)} %obj_ref.3), custom_call_target="tpu_custom_call" | custom-call | tf_op jit(solution)/shard_map/pallas_call | solution.py:591
  12.3 10.4 %shard_map.113 = (f32[1,2,512,512]{3,2,1,0:T(8,128)}, bf16[2,64,512]{2,1,0:T(8,128)(2,1)}, bf16[512,128]{1,0:T(8,128)(2,1)}, bf16[64,128]{1,0:T(8,128)(2,1)}, bf...) custom-call(s32[1,1,1,2,2]{4,3,2,1,0:T(2,128)} %pos_ref.1, ...), custom_call_target="tpu_custom_call" | custom-call | tf_op jit(solution)/shard_map/pallas_call | solution.py:603
  22.7 32.7 %shard_map.114 = (bf16[2,64,512]{2,1,0:T(8,128)(2,1)}, bf16[512,128]{1,0:T(8,128)(2,1)}, bf16[64,128]{1,0:T(8,128)(2,1)}, bf16[2,4,128,256]{3,2,1,0:T(8,128)(2,1)}, bf16[128,8,256]{2,1,0:T(8,128)(2,1)}) custom-call(bf16[1152,640]{1,0:T(8,128)(2,1)} %get-tuple-element.25.sino_ref, bf16[2,64,512]{2,1,0:T(8,128)(2,1)} %get-tuple-element.26.row_ref, ...), custom_call_target="tpu_custom_call" | custom-call | tf_op jit(solution)/shard_map/pallas_call | solution.py:637
  55.4 3.5 %shard_map.115 = (f32[1,2,512,512]{3,2,1,0:T(8,128)}, f32[1,2,2,256,256]{4,3,2,1,0:T(8,128)}, f32[1,4,2,1024]{3,2,1,0:T(2,128)}) custom-call(s32[8,16]{1,0:T(8,128)} %bi_ref.3, f32[1,2,512,512]{3,2,1,0:T(8,128)} %get-tuple-element.24.og_ref, bf16[2,64,512]{2,1,0:T(8,128)(2,1)} %get-tuple-element.32.row_ref, ...), custom_call_target="tpu_custom_call", output_to_operand_aliasing={{0}: (1, {})} | custom-call | tf_op jit(solution)/shard_map/pallas_call | solution.py:664

commit v5 on v4

--- a/solution.py
+++ b/solution.py
@@ -48,7 +48,7 @@
 
 
 def strips_kernel(
-    angles, bi_ref, obj_ref, named_out, row_out, col_out, cor_out, block, packed, load_sem, send_sem, recv_sem,
+    obj_ref, row_out, col_out, cor_out, block, packed, load_sem, send_sem, recv_sem,
 ):
     ang, sy, sx = lax.axis_index("ang"), lax.axis_index("sy"), lax.axis_index("sx")
     oy, ox = 1 - sy, 1 - sx
@@ -77,31 +77,18 @@
     ]
     for copy in copies:
         copy.start()
-    named = [(jnp.int32(-1), jnp.int32(0)), (jnp.int32(0), jnp.int32(0))]
-    for j in range(2 * angles):
-        entry = bi_ref[j // 16, j % 16]
-        mine = (entry >> 3) == ang
-        early = jnp.logical_and(mine, named[0][0] < 0)
-        named = [
-            (jnp.where(take, j, at), jnp.where(take, entry & 7, column))
-            for take, (at, column) in zip((early, mine), named)
-        ]
-    named[0] = (jnp.maximum(named[0][0], 0), named[0][1])
-    for s, (entry, column) in enumerate(named):
-        named_out[2 * s] = entry
-        named_out[2 * s + 1] = column
     for copy in copies:
         copy.wait()
 
 
 def patch_kernel(
     angles,
-    pos_ref, named_ref,
+    pos_ref, bi_ref,
     obj_ref, halo_row, halo_col, halo_cor, probe_ref, data_ref, fwd_ref, bwd_ref, ramp_ref, bv_ref,
-    og_out, row_out, col_out, cor_out, part_out, ramp_out, bv_out, sino_out,
+    og_out, row_out, col_out, cor_out, part_out, msgs_out, over_out, edge_out,
     big, side, probe, data, fwd, bwd, ramp, bv,
     win, patch, exits, half, far, chi, placed, og,
-    rim_row, rim_col, rim_cor, part, sino,
+    rim_row, rim_col, rim_cor, part, sino, lines, over_send, edge_send, msgs,
     load_sem, pick_sem, out_sem, piece_sem,
 ):
     ang, sy, sx = lax.axis_index("ang"), lax.axis_index("sy"), lax.axis_index("sx")
@@ -134,7 +121,16 @@
         placed[q, 0, RIM : RIM + PATCH, :] = jnp.zeros((PATCH, BLK), F32)
         placed[q, 4, RIM : RIM + PATCH, :] = jnp.zeros((PATCH, BLK), F32)
 
-    named = [(named_ref[0], named_ref[1]), (named_ref[2], named_ref[3])]
+    named = [(jnp.int32(-1), jnp.int32(0)), (jnp.int32(0), jnp.int32(0))]
+    for j in range(2 * angles):
+        entry = bi_ref[j // 16, j % 16]
+        mine = (entry >> 3) == ang
+        early = jnp.logical_and(mine, named[0][0] < 0)
+        named = [
+            (jnp.where(take, j, at), jnp.where(take, entry & 7, column))
+            for take, (at, column) in zip((early, mine), named)
+        ]
+    named[0] = (jnp.maximum(named[0][0], 0), named[0][1])
     picks = []
     for s, (entry, column) in enumerate(named):
         at = pl.multiple_of((7 - column + 3 * sx) * BLK, BLK)
@@ -272,7 +268,7 @@
         for i, (src, dst) in enumerate(
             [
                 (rim_row, row_out), (rim_col, col_out), (rim_cor, cor_out),
-                (part, part_out), (ramp, ramp_out), (bv, bv_out),
+                (part, part_out), (msgs, msgs_out), (over_send, over_out), (edge_send, edge_out),
             ]
         )
     ]
@@ -280,8 +276,6 @@
         copy.start()
     for copy in picks:
         copy.wait()
-    for copy in outs[4:6]:
-        copy.start()
 
     for c in range(2):
         for b in range(5):
@@ -289,17 +283,9 @@
                 c, rim_chunk, b + ox
             ).astype(BF)
 
-    over_rows = pl.ds(2 * TILE, 2 * RIM)
-    over_copy = pltpu.make_async_copy(sino.at[over_rows], sino_out.at[over_rows], out_sem.at[6])
-    over_copy.start()
-
     def finished(r):
         rows = pl.ds(pl.multiple_of(r * RIM, RIM), RIM)
-        spans = [pl.ds(pl.multiple_of(c * TILE + r * RIM, RIM), RIM) for c in range(2)]
-        return [pltpu.make_async_copy(og.at[:, rows], og_out.at[0, :, rows], piece_sem.at[r, 2])] + [
-            pltpu.make_async_copy(sino.at[spans[c]], sino_out.at[spans[c]], piece_sem.at[r, c])
-            for c in range(2)
-        ]
+        return pltpu.make_async_copy(og.at[:, rows], og_out.at[0, :, rows], piece_sem.at[r])
 
     def interior(r, carry):
         rows = pl.ds(pl.multiple_of(r * RIM, RIM), RIM)
@@ -310,8 +296,7 @@
                 sino[pl.ds(pl.multiple_of(c * TILE + r * RIM, RIM), RIM), b * BLK : (b + 1) * BLK] = cells_at(
                     c, r + 1, b + ox
                 ).astype(BF)
-        for copy in finished(r):
-            copy.start()
+        finished(r).start()
         return carry
 
     lax.fori_loop(0, 8, interior, 0)
@@ -326,24 +311,37 @@
             part[0, q] = terms[0:BLK].astype(BF)
             part[1, SECOND[q]] = terms[BLK:].astype(BF)
     outs[3].start()
+    for s in range(2):
+        filtered = jnp.dot(sino[...], ramp[s], preferred_element_type=F32).astype(BF)
+        lines[s] = jnp.dot(filtered, bv[s], preferred_element_type=F32)
+        for c in range(2):
+            over_send[s, c] = lines[s, 2 * TILE + c * RIM : 2 * TILE + (c + 1) * RIM, :].astype(BF)
+            edge_send[s, c] = lines[s, pl.ds(pl.multiple_of(c * TILE + (TILE - RIM) * oy, RIM), RIM), :]
+    top = lax.broadcasted_iota(jnp.int32, (64, 8, BLK), 1) < 4
+    for s in range(2):
+        a = lines[s, 0:TILE, :].reshape(64, 8, BLK)
+        b = lines[s, TILE : 2 * TILE, :].reshape(64, 8, BLK)
+        lanes = slice(s * BLK, (s + 1) * BLK)
+        msgs[:, 0, :, lanes] = jnp.where(top, a, pltpu.roll(b, 4, 1)).astype(BF)
+        msgs[:, 1, :, lanes] = jnp.where(top, pltpu.roll(a, 4, 1), b).astype(BF)
+    for copy in outs[4:]:
+        copy.start()
 
     def settle(r, carry):
-        for copy in finished(r):
-            copy.wait()
+        finished(r).wait()
         return carry
 
     lax.fori_loop(0, 8, settle, 0)
     for copy in outs:
         copy.wait()
-    over_copy.wait()
 
 
 def regroup_kernel(
     angles,
-    sino_ref, row_ref, col_ref, cor_ref, part_ref, ramp_ref, bv_ref,
+    msgs_ref, over_ref, edge_ref, row_ref, col_ref, cor_ref, part_ref,
     got_row, got_col, got_cor, total_out, inbox_out,
-    sino, part, ramp, bv, part_got, part_sum, quarter_send, quarter_got, total,
-    lines, over_send, over_got, msgs, inbox,
+    part, part_got, part_sum, quarter_send, quarter_got, total,
+    edges, over_got, last_msgs, inbox,
     load_sem, rim_send, rim_recv, part_ssem, part_rsem, over_ssem, over_rsem,
     word_sem, a2a_send, a2a_recv, own_sem, out_sem,
 ):
@@ -372,7 +370,7 @@
     loads = [
         pltpu.make_async_copy(src, dst, load_sem.at[i])
         for i, (src, dst) in enumerate(
-            [(sino_ref, sino), (ramp_ref, ramp), (bv_ref, bv)]
+            [(edge_ref, edges)]
             + [(part_ref.at[h, pl.ds(routes[h][2], 2)], part.at[h]) for h in range(2)]
         )
     ]
@@ -393,50 +391,39 @@
         exchange(0, h, part_ref.at[h, pl.ds(routes[h][3], 2)], part_got.at[h], routes[h][0])
         for h in range(2)
     ]
-    for copy in firsts:
-        copy.start()
-    for copy in loads:
-        copy.wait()
-
-    for s in range(2):
-        filtered = jnp.dot(sino[...], ramp[s], preferred_element_type=F32).astype(BF)
-        lines[s] = jnp.dot(filtered, bv[s], preferred_element_type=F32)
-        for c in range(2):
-            over_send[s, c] = lines[s, 2 * TILE + c * RIM : 2 * TILE + (c + 1) * RIM, :].astype(BF)
     over = pltpu.make_async_remote_copy(
-        src_ref=over_send, dst_ref=over_got, send_sem=over_ssem, recv_sem=over_rsem,
+        src_ref=over_ref, dst_ref=over_got, send_sem=over_ssem, recv_sem=over_rsem,
         device_id=(ang, oy, sx), device_id_type=MESH,
     )
     over.start()
-    top = lax.broadcasted_iota(jnp.int32, (64, 8, BLK), 1) < 4
-    for s in range(2):
-        a = lines[s, 0:TILE, :].reshape(64, 8, BLK)
-        b = lines[s, TILE : 2 * TILE, :].reshape(64, 8, BLK)
-        lanes = slice(s * BLK, (s + 1) * BLK)
-        msgs[:, 0, :, lanes] = jnp.where(top, a, pltpu.roll(b, 4, 1)).astype(BF)
-        msgs[:, 1, :, lanes] = jnp.where(top, pltpu.roll(a, 4, 1), b).astype(BF)
-
-    def send_to(d):
+    for copy in firsts:
+        copy.start()
+    top = lax.broadcasted_iota(jnp.int32, (8, 8, BLK), 1) < 4
+
+    def send_to(src, d):
         @pl.when(d != me)
         def _():
             pltpu.make_async_remote_copy(
-                src_ref=msgs.at[d >> 1, d & 1], dst_ref=inbox.at[me],
-                send_sem=a2a_send, recv_sem=a2a_recv,
+                src_ref=src, dst_ref=inbox.at[me], send_sem=a2a_send, recv_sem=a2a_recv,
                 device_id=(d >> 1, sy, d & 1), device_id_type=MESH,
             ).start()
 
     inner = group - 16
 
     def send_inner(k, carry):
-        send_to(16 * sy + lax.rem(me + k, inner))
+        d = 16 * sy + lax.rem(me + k, inner)
+        send_to(msgs_ref.at[d >> 1, d & 1], d)
         return carry
 
     def send_edge(k, carry):
-        send_to(inner * oy + ((me + k) & 15))
+        e = (me + k) & 15
+        send_to(last_msgs.at[e >> 1, e & 1], inner * oy + e)
         return carry
 
     pl.semaphore_wait(word_sem, len(crosswise))
     lax.fori_loop(0, inner // 2, send_inner, 0)
+    for copy in loads:
+        copy.wait()
     seconds = []
     for h, (_, after, _, _, keep, give) in enumerate(routes):
         firsts[h].wait()
@@ -446,18 +433,25 @@
         seconds[h].start()
     lax.fori_loop(inner // 2, inner, send_inner, 0)
     over.wait()
-    edge = pl.ds(pl.multiple_of((TILE - RIM) * oy, RIM), RIM)
-    edge_low = pl.ds(pl.multiple_of(TILE + (TILE - RIM) * oy, RIM), RIM)
-    pairs = pl.ds(56 * oy, 8)
     for s in range(2):
-        a = (lines[s, edge, :] + over_got[s, 0].astype(F32)).reshape(8, 8, BLK)
-        b = (lines[s, edge_low, :] + over_got[s, 1].astype(F32)).reshape(8, 8, BLK)
+        a = (edges[s, 0] + over_got[s, 0].astype(F32)).reshape(8, 8, BLK)
+        b = (edges[s, 1] + over_got[s, 1].astype(F32)).reshape(8, 8, BLK)
         lanes = slice(s * BLK, (s + 1) * BLK)
-        msgs[pairs, 0, :, lanes] = jnp.where(top[0:8], a, pltpu.roll(b, 4, 1)).astype(BF)
-        msgs[pairs, 1, :, lanes] = jnp.where(top[0:8], pltpu.roll(a, 4, 1), b).astype(BF)
+        last_msgs[:, 0, :, lanes] = jnp.where(top, a, pltpu.roll(b, 4, 1)).astype(BF)
+        last_msgs[:, 1, :, lanes] = jnp.where(top, pltpu.roll(a, 4, 1), b).astype(BF)
     lax.fori_loop(0, 16, send_edge, 0)
-    own = pltpu.make_async_copy(msgs.at[ang, sx], inbox.at[me], own_sem)
-    own.start()
+    own = pltpu.make_async_copy(msgs_ref.at[ang, sx], inbox.at[me], own_sem)
+    own_last = pltpu.make_async_copy(last_msgs.at[(me & 15) >> 1, sx], inbox.at[me], own_sem)
+    at_edge = jnp.logical_and(me >= inner * oy, me < inner * oy + 16)
+
+    @pl.when(at_edge)
+    def _():
+        own_last.start()
+
+    @pl.when(jnp.logical_not(at_edge))
+    def _():
+        own.start()
+
 
     thirds = []
     for h, (_, after, base, _, keep, _) in enumerate(routes):
@@ -588,23 +582,23 @@
         return jax.ShapeDtypeStruct(dims, kind)
 
     rim_shapes = (shape((2, RIM, TILE), BF), shape((TILE, BLK), BF), shape((RIM, BLK), BF))
-    named, *halos = pl.pallas_call(
-        functools.partial(strips_kernel, angles),
-        out_shape=(shape((4,), jnp.int32),) + rim_shapes,
-        in_specs=[smem, hbm],
-        out_specs=[smem] + [hbm] * 3,
+    halos = pl.pallas_call(
+        strips_kernel,
+        out_shape=rim_shapes,
+        in_specs=[hbm],
+        out_specs=[hbm] * 3,
         scratch_shapes=[
             pltpu.VMEM((2, TILE, BLK), BF), pltpu.VMEM((TILE, BLK), BF), dma, dma((3,)), dma((3,)),
         ],
         compiler_params=pltpu.CompilerParams(
             collective_id=0, has_side_effects=True, vmem_limit_bytes=62 * 1024 * 1024
         ),
-    )(block_index, objects)
-    og_part, row, col, cor, parts, ramp_two, bv_two, sino = pl.pallas_call(
+    )(objects)
+    og_part, row, col, cor, parts, messages, over, edges = pl.pallas_call(
         functools.partial(patch_kernel, angles),
         out_shape=(shape((1, 2, TILE, TILE), F32),) + rim_shapes + (
-            shape((2, 4, BLK, PATCH), BF), shape((2, SPAN, BLK), BF), shape((2, BLK, BLK), BF),
-            shape((2 * ROWS - 2 * RIM, SPAN), BF),
+            shape((2, 4, BLK, PATCH), BF), shape((group // 2, 2, 8, 2 * BLK), BF),
+            shape((2, 2, RIM, BLK), BF), shape((2, 2, RIM, BLK), F32),
         ),
         in_specs=[smem] * 2 + [hbm] * 10,
         out_specs=[hbm] * 8,
@@ -630,37 +624,37 @@
             pltpu.VMEM((RIM, BLK), BF),
             pltpu.VMEM((2, 4, BLK, PATCH), BF),
             pltpu.VMEM((2 * ROWS - 2 * RIM, SPAN), BF),
-            dma((8,)), dma((4,)), dma((7,)), dma((8, 3)),
+            pltpu.VMEM((2, 2 * ROWS - 2 * RIM, BLK), F32),
+            pltpu.VMEM((2, 2, RIM, BLK), BF),
+            pltpu.VMEM((2, 2, RIM, BLK), F32),
+            pltpu.VMEM((group // 2, 2, 8, 2 * BLK), BF),
+            dma((8,)), dma((4,)), dma((7,)), dma((8,)),
         ],
         compiler_params=pltpu.CompilerParams(vmem_limit_bytes=62 * 1024 * 1024),
-    )(positions, named, objects, *halos, probe, data, forward, backward, ramp, block_values)
+    )(positions, block_index, objects, *halos, probe, data, forward, backward, ramp, block_values)
     got_row, got_col, got_cor, total, inbox = pl.pallas_call(
         functools.partial(regroup_kernel, angles),
         out_shape=rim_shapes + (shape((2, 4, BLK, PATCH), BF), shape((group, 8, 2 * BLK), BF)),
         in_specs=[hbm] * 7,
         out_specs=[hbm] * 5,
         scratch_shapes=[
-            pltpu.VMEM((2 * ROWS - 2 * RIM, SPAN), BF),
             pltpu.VMEM((2, 2, BLK, PATCH), BF),
-            pltpu.VMEM((2, SPAN, BLK), BF),
-            pltpu.VMEM((2, BLK, BLK), BF),
             pltpu.VMEM((2, 2, BLK, PATCH), BF),
             pltpu.VMEM((2, 2, BLK, PATCH), F32),
             pltpu.VMEM((2, BLK, PATCH), BF),
             pltpu.VMEM((2, BLK, PATCH), BF),
             pltpu.VMEM((2, 4, BLK, PATCH), BF),
-            pltpu.VMEM((2, 2 * ROWS - 2 * RIM, BLK), F32),
+            pltpu.VMEM((2, 2, RIM, BLK), F32),
             pltpu.VMEM((2, 2, RIM, BLK), BF),
-            pltpu.VMEM((2, 2, RIM, BLK), BF),
-            pltpu.VMEM((group // 2, 2, 8, 2 * BLK), BF),
+            pltpu.VMEM((8, 2, 8, 2 * BLK), BF),
             pltpu.VMEM((group, 8, 2 * BLK), BF),
-            dma((5,)), dma((3,)), dma((3,)), dma((4, 2)), dma((4, 2)), dma, dma,
+            dma((3,)), dma((3,)), dma((3,)), dma((4, 2)), dma((4, 2)), dma, dma,
             pltpu.SemaphoreType.REGULAR, dma, dma, dma, dma((2,)),
         ],
         compiler_params=pltpu.CompilerParams(
             collective_id=1, has_side_effects=True, vmem_limit_bytes=62 * 1024 * 1024
         ),
-    )(sino, row, col, cor, parts, ramp_two, bv_two)
+    )(messages, over, edges, row, col, cor, parts)
     return pl.pallas_call(
         functools.partial(finish_kernel, angles),
         out_shape=(

time: 59.2 us -> 61.3 us (1.035); the launches traced: 58.9 us -> 60.4 us
  Pallas kernels: 58.3 us -> 59.7 us
    pallas_call x1, Pallas kernels: 10.4 us -> 12.4 us  [body(): pl.pallas_call(functools.partial(patch_kernel, angles), out_shape=(shape(...]
    pallas_call x1, Pallas kernels: 11.6 us -> 10.4 us  [body(): pl.pallas_call(strips_kernel, out_shape=rim_shapes, in_specs=[hbm], out_s...]
    pallas_call x1, Pallas kernels: 32.7 us -> 33.4 us  [body(): pl.pallas_call(functools.partial(regroup_kernel, angles), out_shape=rim_s...]
where the time goes in v5:
time: 61.3 us; the launch traced here: 60.4 us
  Pallas kernels  59.7 us (97%)
  between operations  0.65 us (1%)
    pallas_call x1, Pallas kernels, body(): pl.pallas_call(functools.partial(regroup_kernel, angles), out_shape=rim_s...  33.4 us
    pallas_call x1, Pallas kernels, body(): pl.pallas_call(functools.partial(patch_kernel, angles), out_shape=(shape(...  12.4 us
    pallas_call x1, Pallas kernels, body(): pl.pallas_call(strips_kernel, out_shape=rim_shapes, in_specs=[hbm], out_s...  10.4 us
    pallas_call x1, Pallas kernels, body(): pl.pallas_call(functools.partial(finish_kernel, angles), out_shape=(shape...  3.54 us

profile of v5, /device:TPU:1, one launch (start us, length us, event | category | flops | bytes accessed | tf_op | source)
XLA Modules:
  0.0 60.4 jit_solution(14722622616884736773)
XLA Ops:
  0.6 10.4 %shard_map.112 = (bf16[2,64,512]{2,1,0:T(8,128)(2,1)}, bf16[512,128]{1,0:T(8,128)(2,1)}, bf16[64,128]{1,0:T(8,128)(2,1)}) custom-call(bf16[1,2,512,512]{3,2,1,0:T(8,128)(2,1)} %obj_ref.3), custom_call_target="tpu_custom_call" | custom-call | tf_op jit(solution)/shard_map/pallas_call | solution.py:585
  11.0 12.4 %shard_map.113 = (f32[1,2,512,512]{3,2,1,0:T(8,128)}, bf16[2,64,512]{2,1,0:T(8,128)(2,1)}, bf16[512,128]{1,0:T(8,128)(2,1)}, bf16[64,128]{1,0:T(8,128)(2,1)}, bf...) custom-call(s32[1,1,1,2,2]{4,3,2,1,0:T(2,128)} %pos_ref.1, ...), custom_call_target="tpu_custom_call" | custom-call | tf_op jit(solution)/shard_map/pallas_call | solution.py:597
  23.5 33.4 %shard_map.114 = (bf16[2,64,512]{2,1,0:T(8,128)(2,1)}, bf16[512,128]{1,0:T(8,128)(2,1)}, bf16[64,128]{1,0:T(8,128)(2,1)}, bf16[2,4,128,256]{3,2,1,0:T(8,128)(2,1)}, bf16[128,8,256]{2,1,0:T(8,128)(2,1)}) custom-call(bf16[64,2,8,256]{3,2,1,0:T(8,128)(2,1)} %get-tuple-element.23.msgs_ref, bf16[2,2,64,128]{3,2,1,0:T(8,128)(2,1)} %get-tuple-element.24.over_ref, ...), custom_call_target="tpu_custom_call" | custom-call | tf_op jit(solution)/shard_map/pallas_call | solution.py:635
  56.9 3.5 %shard_map.115 = (f32[1,2,512,512]{3,2,1,0:T(8,128)}, f32[1,2,2,256,256]{4,3,2,1,0:T(8,128)}, f32[1,4,2,1024]{3,2,1,0:T(2,128)}) custom-call(s32[8,16]{1,0:T(8,128)} %bi_ref.3, f32[1,2,512,512]{3,2,1,0:T(8,128)} %get-tuple-element.22.og_ref, bf16[2,64,512]{2,1,0:T(8,128)(2,1)} %get-tuple-element.30.row_ref, ...), custom_call_target="tpu_custom_call", output_to_operand_aliasing={{0}: (1, {})} | custom-call | tf_op jit(solution)/shard_map/pallas_call | solution.py:658

commit v6 on v4

--- a/solution.py
+++ b/solution.py
@@ -48,7 +48,7 @@
 
 
 def strips_kernel(
-    angles, bi_ref, obj_ref, named_out, row_out, col_out, cor_out, block, packed, load_sem, send_sem, recv_sem,
+    obj_ref, row_out, col_out, cor_out, block, packed, load_sem, send_sem, recv_sem,
 ):
     ang, sy, sx = lax.axis_index("ang"), lax.axis_index("sy"), lax.axis_index("sx")
     oy, ox = 1 - sy, 1 - sx
@@ -77,26 +77,13 @@
     ]
     for copy in copies:
         copy.start()
-    named = [(jnp.int32(-1), jnp.int32(0)), (jnp.int32(0), jnp.int32(0))]
-    for j in range(2 * angles):
-        entry = bi_ref[j // 16, j % 16]
-        mine = (entry >> 3) == ang
-        early = jnp.logical_and(mine, named[0][0] < 0)
-        named = [
-            (jnp.where(take, j, at), jnp.where(take, entry & 7, column))
-            for take, (at, column) in zip((early, mine), named)
-        ]
-    named[0] = (jnp.maximum(named[0][0], 0), named[0][1])
-    for s, (entry, column) in enumerate(named):
-        named_out[2 * s] = entry
-        named_out[2 * s + 1] = column
     for copy in copies:
         copy.wait()
 
 
 def patch_kernel(
     angles,
-    pos_ref, named_ref,
+    pos_ref, bi_ref,
     obj_ref, halo_row, halo_col, halo_cor, probe_ref, data_ref, fwd_ref, bwd_ref, ramp_ref, bv_ref,
     og_out, row_out, col_out, cor_out, part_out, ramp_out, bv_out, sino_out,
     big, side, probe, data, fwd, bwd, ramp, bv,
@@ -134,7 +121,16 @@
         placed[q, 0, RIM : RIM + PATCH, :] = jnp.zeros((PATCH, BLK), F32)
         placed[q, 4, RIM : RIM + PATCH, :] = jnp.zeros((PATCH, BLK), F32)
 
-    named = [(named_ref[0], named_ref[1]), (named_ref[2], named_ref[3])]
+    named = [(jnp.int32(-1), jnp.int32(0)), (jnp.int32(0), jnp.int32(0))]
+    for j in range(2 * angles):
+        entry = bi_ref[j // 16, j % 16]
+        mine = (entry >> 3) == ang
+        early = jnp.logical_and(mine, named[0][0] < 0)
+        named = [
+            (jnp.where(take, j, at), jnp.where(take, entry & 7, column))
+            for take, (at, column) in zip((early, mine), named)
+        ]
+    named[0] = (jnp.maximum(named[0][0], 0), named[0][1])
     picks = []
     for s, (entry, column) in enumerate(named):
         at = pl.multiple_of((7 - column + 3 * sx) * BLK, BLK)
@@ -445,6 +441,20 @@
         seconds.append(exchange(1, h, quarter_send.at[h], quarter_got.at[h], after))
         seconds[h].start()
     lax.fori_loop(inner // 2, inner, send_inner, 0)
+    rims = [
+        pltpu.make_async_remote_copy(
+            src_ref=src, dst_ref=dst, send_sem=rim_send.at[i], recv_sem=rim_recv.at[i],
+            device_id=dev, device_id_type=MESH,
+        )
+        for i, (src, dst, dev) in enumerate(
+            [
+                (row_ref, got_row, (ang, oy, sx)),
+                (col_ref, got_col, beside),
+                (cor_ref, got_cor, across),
+            ]
+        )
+    ]
+    rims[0].start()
     over.wait()
     edge = pl.ds(pl.multiple_of((TILE - RIM) * oy, RIM), RIM)
     edge_low = pl.ds(pl.multiple_of(TILE + (TILE - RIM) * oy, RIM), RIM)
@@ -466,21 +476,8 @@
         total[h, base + keep] = (part_sum[h, keep] + quarter_got[h].astype(F32)).astype(BF)
         thirds.append(exchange(2, h, at, at, after))
         thirds[h].start()
-    rims = [
-        pltpu.make_async_remote_copy(
-            src_ref=src, dst_ref=dst, send_sem=rim_send.at[i], recv_sem=rim_recv.at[i],
-            device_id=dev, device_id_type=MESH,
-        )
-        for i, (src, dst, dev) in enumerate(
-            [
-                (row_ref, got_row, (ang, oy, sx)),
-                (col_ref, got_col, beside),
-                (cor_ref, got_cor, across),
-            ]
-        )
-    ]
-    for copy in rims:
-        copy.start()
+    rims[1].start()
+    rims[2].start()
     fourths = []
     for h, (before, _, base, _, _, _) in enumerate(routes):
         thirds[h].wait()
@@ -588,18 +585,18 @@
         return jax.ShapeDtypeStruct(dims, kind)
 
     rim_shapes = (shape((2, RIM, TILE), BF), shape((TILE, BLK), BF), shape((RIM, BLK), BF))
-    named, *halos = pl.pallas_call(
-        functools.partial(strips_kernel, angles),
-        out_shape=(shape((4,), jnp.int32),) + rim_shapes,
-        in_specs=[smem, hbm],
-        out_specs=[smem] + [hbm] * 3,
+    halos = pl.pallas_call(
+        strips_kernel,
+        out_shape=rim_shapes,
+        in_specs=[hbm],
+        out_specs=[hbm] * 3,
         scratch_shapes=[
             pltpu.VMEM((2, TILE, BLK), BF), pltpu.VMEM((TILE, BLK), BF), dma, dma((3,)), dma((3,)),
         ],
         compiler_params=pltpu.CompilerParams(
             collective_id=0, has_side_effects=True, vmem_limit_bytes=62 * 1024 * 1024
         ),
-    )(block_index, objects)
+    )(objects)
     og_part, row, col, cor, parts, ramp_two, bv_two, sino = pl.pallas_call(
         functools.partial(patch_kernel, angles),
         out_shape=(shape((1, 2, TILE, TILE), F32),) + rim_shapes + (
@@ -633,7 +630,7 @@
             dma((8,)), dma((4,)), dma((7,)), dma((8, 3)),
         ],
         compiler_params=pltpu.CompilerParams(vmem_limit_bytes=62 * 1024 * 1024),
-    )(positions, named, objects, *halos, probe, data, forward, backward, ramp, block_values)
+    )(positions, block_index, objects, *halos, probe, data, forward, backward, ramp, block_values)
     got_row, got_col, got_cor, total, inbox = pl.pallas_call(
         functools.partial(regroup_kernel, angles),
         out_shape=rim_shapes + (shape((2, 4, BLK, PATCH), BF), shape((group, 8, 2 * BLK), BF)),

time: 59.2 us -> 58.2 us (0.983)
  Pallas kernels: 58.3 us -> 57.3 us
    pallas_call x1, Pallas kernels: 11.6 us -> 10.4 us  [body(): pl.pallas_call(strips_kernel, out_shape=rim_shapes, in_specs=[hbm], out_s...]
where the time goes in v6:
time: 58.2 us; the launch traced here: 58 us
  Pallas kernels  57.3 us (98%)
  between operations  0.65 us (1%)
    pallas_call x1, Pallas kernels, body(): pl.pallas_call(functools.partial(regroup_kernel, angles), out_shape=rim_s...  32.9 us
    pallas_call x1, Pallas kernels, body(): pl.pallas_call(functools.partial(patch_kernel, angles), out_shape=(shape(...  10.5 us
    pallas_call x1, Pallas kernels, body(): pl.pallas_call(strips_kernel, out_shape=rim_shapes, in_specs=[hbm], out_s...  10.4 us
    pallas_call x1, Pallas kernels, body(): pl.pallas_call(functools.partial(finish_kernel, angles), out_shape=(shape...  3.54 us

profile of v6, /device:TPU:1, one launch (start us, length us, event | category | flops | bytes accessed | tf_op | source)
XLA Modules:
  0.0 58.0 jit_solution(17144357225354777367)
XLA Ops:
  0.6 10.4 %shard_map.112 = (bf16[2,64,512]{2,1,0:T(8,128)(2,1)}, bf16[512,128]{1,0:T(8,128)(2,1)}, bf16[64,128]{1,0:T(8,128)(2,1)}) custom-call(bf16[1,2,512,512]{3,2,1,0:T(8,128)(2,1)} %obj_ref.3), custom_call_target="tpu_custom_call" | custom-call | tf_op jit(solution)/shard_map/pallas_call | solution.py:588
  11.0 10.5 %shard_map.113 = (f32[1,2,512,512]{3,2,1,0:T(8,128)}, bf16[2,64,512]{2,1,0:T(8,128)(2,1)}, bf16[512,128]{1,0:T(8,128)(2,1)}, bf16[64,128]{1,0:T(8,128)(2,1)}, bf...) custom-call(s32[1,1,1,2,2]{4,3,2,1,0:T(2,128)} %pos_ref.1, ...), custom_call_target="tpu_custom_call" | custom-call | tf_op jit(solution)/shard_map/pallas_call | solution.py:600
  21.5 32.9 %shard_map.114 = (bf16[2,64,512]{2,1,0:T(8,128)(2,1)}, bf16[512,128]{1,0:T(8,128)(2,1)}, bf16[64,128]{1,0:T(8,128)(2,1)}, bf16[2,4,128,256]{3,2,1,0:T(8,128)(2,1)}, bf16[128,8,256]{2,1,0:T(8,128)(2,1)}) custom-call(bf16[1152,640]{1,0:T(8,128)(2,1)} %get-tuple-element.23.sino_ref, bf16[2,64,512]{2,1,0:T(8,128)(2,1)} %get-tuple-element.24.row_ref, ...), custom_call_target="tpu_custom_call" | custom-call | tf_op jit(solution)/shard_map/pallas_call | solution.py:634
  54.4 3.5 %shard_map.115 = (f32[1,2,512,512]{3,2,1,0:T(8,128)}, f32[1,2,2,256,256]{4,3,2,1,0:T(8,128)}, f32[1,4,2,1024]{3,2,1,0:T(2,128)}) custom-call(s32[8,16]{1,0:T(8,128)} %bi_ref.3, f32[1,2,512,512]{3,2,1,0:T(8,128)} %get-tuple-element.22.og_ref, bf16[2,64,512]{2,1,0:T(8,128)(2,1)} %get-tuple-element.30.row_ref, ...), custom_call_target="tpu_custom_call", output_to_operand_aliasing={{0}: (1, {})} | custom-call | tf_op jit(solution)/shard_map/pallas_call | solution.py:661

commit v7 on v6

--- a/solution.py
+++ b/solution.py
@@ -339,7 +339,7 @@
     sino_ref, row_ref, col_ref, cor_ref, part_ref, ramp_ref, bv_ref,
     got_row, got_col, got_cor, total_out, inbox_out,
     sino, part, ramp, bv, part_got, part_sum, quarter_send, quarter_got, total,
-    lines, over_send, over_got, msgs, inbox,
+    lines, over_send, over_got, msgs,
     load_sem, rim_send, rim_recv, part_ssem, part_rsem, over_ssem, over_rsem,
     word_sem, a2a_send, a2a_recv, own_sem, out_sem,
 ):
@@ -416,7 +416,7 @@
         @pl.when(d != me)
         def _():
             pltpu.make_async_remote_copy(
-                src_ref=msgs.at[d >> 1, d & 1], dst_ref=inbox.at[me],
+                src_ref=msgs.at[d >> 1, d & 1], dst_ref=inbox_out.at[me],
                 send_sem=a2a_send, recv_sem=a2a_recv,
                 device_id=(d >> 1, sy, d & 1), device_id_type=MESH,
             ).start()
@@ -466,7 +466,7 @@
         msgs[pairs, 0, :, lanes] = jnp.where(top[0:8], a, pltpu.roll(b, 4, 1)).astype(BF)
         msgs[pairs, 1, :, lanes] = jnp.where(top[0:8], pltpu.roll(a, 4, 1), b).astype(BF)
     lax.fori_loop(0, 16, send_edge, 0)
-    own = pltpu.make_async_copy(msgs.at[ang, sx], inbox.at[me], own_sem)
+    own = pltpu.make_async_copy(msgs.at[ang, sx], inbox_out.at[me], own_sem)
     own.start()
 
     thirds = []
@@ -478,29 +478,27 @@
         thirds[h].start()
     rims[1].start()
     rims[2].start()
-    fourths = []
+    fourths, kept = [], []
     for h, (before, _, base, _, _, _) in enumerate(routes):
         thirds[h].wait()
-        at = total.at[h, pl.ds(base, 2)]
-        fourths.append(exchange(3, h, at, at, before))
+        at = pl.ds(base, 2)
+        fourths.append(exchange(3, h, total.at[h, at], total_out.at[h, at], before))
         fourths[h].start()
+        kept.append(pltpu.make_async_copy(total.at[h, at], total_out.at[h, at], out_sem.at[h]))
+        kept[h].start()
     own.wait()
     pltpu.make_async_copy(
-        inbox.at[pl.ds(0, group - 1)], inbox.at[pl.ds(0, group - 1)], a2a_recv
+        inbox_out.at[pl.ds(0, group - 1)], inbox_out.at[pl.ds(0, group - 1)], a2a_recv
     ).wait()
-    inbox_copy = pltpu.make_async_copy(inbox, inbox_out, out_sem.at[0])
-    inbox_copy.start()
     for copy in fourths:
         copy.wait()
-    total_copy = pltpu.make_async_copy(total, total_out, out_sem.at[1])
-    total_copy.start()
     pltpu.make_async_copy(
-        inbox.at[pl.ds(0, group - 1)], inbox.at[pl.ds(0, group - 1)], a2a_send
+        inbox_out.at[pl.ds(0, group - 1)], inbox_out.at[pl.ds(0, group - 1)], a2a_send
     ).wait()
     for copy in rims:
         copy.wait()
-    inbox_copy.wait()
-    total_copy.wait()
+    for copy in kept:
+        copy.wait()
 
 
 def finish_kernel(
@@ -650,7 +648,6 @@
             pltpu.VMEM((2, 2, RIM, BLK), BF),
             pltpu.VMEM((2, 2, RIM, BLK), BF),
             pltpu.VMEM((group // 2, 2, 8, 2 * BLK), BF),
-            pltpu.VMEM((group, 8, 2 * BLK), BF),
             dma((5,)), dma((3,)), dma((3,)), dma((4, 2)), dma((4, 2)), dma, dma,
             pltpu.SemaphoreType.REGULAR, dma, dma, dma, dma((2,)),
         ],

time: 58.2 us -> 57.5 us (0.988)
  Pallas kernels: 57.3 us -> 56.6 us
    pallas_call x1, Pallas kernels: 32.9 us -> 32.2 us  [body(): pl.pallas_call(functools.partial(regroup_kernel, angles), out_shape=rim_s...]
where the time goes in v7:
time: 57.5 us; the launch traced here: 57.3 us
  Pallas kernels  56.6 us (98%)
  between operations  0.65 us (1%)
    pallas_call x1, Pallas kernels, body(): pl.pallas_call(functools.partial(regroup_kernel, angles), out_shape=rim_s...  32.2 us
    pallas_call x1, Pallas kernels, body(): pl.pallas_call(functools.partial(patch_kernel, angles), out_shape=(shape(...  10.5 us
    pallas_call x1, Pallas kernels, body(): pl.pallas_call(strips_kernel, out_shape=rim_shapes, in_specs=[hbm], out_s...  10.4 us
    pallas_call x1, Pallas kernels, body(): pl.pallas_call(functools.partial(finish_kernel, angles), out_shape=(shape...  3.54 us

profile of v7, /device:TPU:1, one launch (start us, length us, event | category | flops | bytes accessed | tf_op | source)
XLA Modules:
  0.0 57.3 jit_solution(15869537014748027795)
XLA Ops:
  0.6 10.4 %shard_map.112 = (bf16[2,64,512]{2,1,0:T(8,128)(2,1)}, bf16[512,128]{1,0:T(8,128)(2,1)}, bf16[64,128]{1,0:T(8,128)(2,1)}) custom-call(bf16[1,2,512,512]{3,2,1,0:T(8,128)(2,1)} %obj_ref.3), custom_call_target="tpu_custom_call" | custom-call | tf_op jit(solution)/shard_map/pallas_call | solution.py:586
  11.0 10.5 %shard_map.113 = (f32[1,2,512,512]{3,2,1,0:T(8,128)}, bf16[2,64,512]{2,1,0:T(8,128)(2,1)}, bf16[512,128]{1,0:T(8,128)(2,1)}, bf16[64,128]{1,0:T(8,128)(2,1)}, bf...) custom-call(s32[1,1,1,2,2]{4,3,2,1,0:T(2,128)} %pos_ref.1, ...), custom_call_target="tpu_custom_call" | custom-call | tf_op jit(solution)/shard_map/pallas_call | solution.py:598
  21.5 32.2 %shard_map.114 = (bf16[2,64,512]{2,1,0:T(8,128)(2,1)}, bf16[512,128]{1,0:T(8,128)(2,1)}, bf16[64,128]{1,0:T(8,128)(2,1)}, bf16[2,4,128,256]{3,2,1,0:T(8,128)(2,1)}, bf16[128,8,256]{2,1,0:T(8,128)(2,1)}) custom-call(bf16[1152,640]{1,0:T(8,128)(2,1)} %get-tuple-element.23.sino_ref, bf16[2,64,512]{2,1,0:T(8,128)(2,1)} %get-tuple-element.24.row_ref, ...), custom_call_target="tpu_custom_call" | custom-call | tf_op jit(solution)/shard_map/pallas_call | solution.py:632
  53.7 3.5 %shard_map.115 = (f32[1,2,512,512]{3,2,1,0:T(8,128)}, f32[1,2,2,256,256]{4,3,2,1,0:T(8,128)}, f32[1,4,2,1024]{3,2,1,0:T(2,128)}) custom-call(s32[8,16]{1,0:T(8,128)} %bi_ref.3, f32[1,2,512,512]{3,2,1,0:T(8,128)} %get-tuple-element.22.og_ref, bf16[2,64,512]{2,1,0:T(8,128)(2,1)} %get-tuple-element.30.row_ref, ...), custom_call_target="tpu_custom_call", output_to_operand_aliasing={{0}: (1, {})} | custom-call | tf_op jit(solution)/shard_map/pallas_call | solution.py:658

commit v8 on v7

--- a/solution.py
+++ b/solution.py
@@ -60,22 +60,23 @@
     barrier = pltpu.get_barrier_semaphore()
     for dev in devices:
         pl.semaphore_signal(barrier, inc=1, device_id=dev, device_id_type=MESH)
+    pl.semaphore_wait(barrier, 3)
+    sources = [obj_ref.at[0, :, rows, :], packed, packed.at[rows]]
+    copies = [
+        pltpu.make_async_remote_copy(
+            src_ref=src, dst_ref=dst, send_sem=send_sem.at[i], recv_sem=recv_sem.at[i],
+            device_id=dev, device_id_type=MESH,
+        )
+        for i, (src, dst, dev) in enumerate(zip(sources, (row_out, col_out, cor_out), devices))
+    ]
+    copies[0].start()
     load.wait()
     real, imag = block[0].astype(F32), block[1].astype(F32)
     low = lax.broadcasted_iota(jnp.int32, (TILE, BLK), 1) < RIM
     packed[...] = jnp.where(
         low, jnp.where(sx == 0, swap_halves(real), real), jnp.where(sx == 0, imag, swap_halves(imag))
     ).astype(BF)
-    pl.semaphore_wait(barrier, 3)
-    sources = [obj_ref.at[0, :, rows, :], packed, packed.at[rows]]
-    copies = [
-        pltpu.make_async_remote_copy(
-            src_ref=src, dst_ref=dst, send_sem=send_sem.at[i], recv_sem=recv_sem.at[i],
-            device_id=dev, device_id_type=MESH,
-        )
-        for i, (src, dst, dev) in enumerate(zip(sources, (row_out, col_out, cor_out), devices))
-    ]
-    for copy in copies:
+    for copy in copies[1:]:
         copy.start()
     for copy in copies:
         copy.wait()

time: 57.5 us -> 57.5 us (level)
  no operation moved by 1% of the time
where the time goes in v8:
time: 57.5 us; the launch traced here: 57.3 us
  Pallas kernels  56.7 us (99%)
  between operations  0.65 us (1%)
    pallas_call x1, Pallas kernels, body(): pl.pallas_call(functools.partial(regroup_kernel, angles), out_shape=rim_s...  32.3 us
    pallas_call x1, Pallas kernels, body(): pl.pallas_call(functools.partial(patch_kernel, angles), out_shape=(shape(...  10.5 us
    pallas_call x1, Pallas kernels, body(): pl.pallas_call(strips_kernel, out_shape=rim_shapes, in_specs=[hbm], out_s...  10.4 us
    pallas_call x1, Pallas kernels, body(): pl.pallas_call(functools.partial(finish_kernel, angles), out_shape=(shape...  3.54 us

profile of v8, /device:TPU:1, one launch (start us, length us, event | category | flops | bytes accessed | tf_op | source)
XLA Modules:
  0.0 57.3 jit_solution(7757561318752074985)
XLA Ops:
  0.6 10.4 %shard_map.112 = (bf16[2,64,512]{2,1,0:T(8,128)(2,1)}, bf16[512,128]{1,0:T(8,128)(2,1)}, bf16[64,128]{1,0:T(8,128)(2,1)}) custom-call(bf16[1,2,512,512]{3,2,1,0:T(8,128)(2,1)} %obj_ref.3), custom_call_target="tpu_custom_call" | custom-call | tf_op jit(solution)/shard_map/pallas_call | solution.py:587
  11.0 10.5 %shard_map.113 = (f32[1,2,512,512]{3,2,1,0:T(8,128)}, bf16[2,64,512]{2,1,0:T(8,128)(2,1)}, bf16[512,128]{1,0:T(8,128)(2,1)}, bf16[64,128]{1,0:T(8,128)(2,1)}, bf...) custom-call(s32[1,1,1,2,2]{4,3,2,1,0:T(2,128)} %pos_ref.1, ...), custom_call_target="tpu_custom_call" | custom-call | tf_op jit(solution)/shard_map/pallas_call | solution.py:599
  21.5 32.3 %shard_map.114 = (bf16[2,64,512]{2,1,0:T(8,128)(2,1)}, bf16[512,128]{1,0:T(8,128)(2,1)}, bf16[64,128]{1,0:T(8,128)(2,1)}, bf16[2,4,128,256]{3,2,1,0:T(8,128)(2,1)}, bf16[128,8,256]{2,1,0:T(8,128)(2,1)}) custom-call(bf16[1152,640]{1,0:T(8,128)(2,1)} %get-tuple-element.23.sino_ref, bf16[2,64,512]{2,1,0:T(8,128)(2,1)} %get-tuple-element.24.row_ref, ...), custom_call_target="tpu_custom_call" | custom-call | tf_op jit(solution)/shard_map/pallas_call | solution.py:633
  53.8 3.5 %shard_map.115 = (f32[1,2,512,512]{3,2,1,0:T(8,128)}, f32[1,2,2,256,256]{4,3,2,1,0:T(8,128)}, f32[1,4,2,1024]{3,2,1,0:T(2,128)}) custom-call(s32[8,16]{1,0:T(8,128)} %bi_ref.3, f32[1,2,512,512]{3,2,1,0:T(8,128)} %get-tuple-element.22.og_ref, bf16[2,64,512]{2,1,0:T(8,128)(2,1)} %get-tuple-element.30.row_ref, ...), custom_call_target="tpu_custom_call", output_to_operand_aliasing={{0}: (1, {})} | custom-call | tf_op jit(solution)/shard_map/pallas_call | solution.py:659
